TPU v7x, 1024 devices: a whole 8x8x8 slice. The times are simulated.
1024 devices in a mesh: lev: 16 (over y, core), lat: 64 (over x, z).
Axes of the slice: x: 8, y: 8, z: 8, core: 2. Of those that a mesh axis runs over, the one named last changes fastest.
Arguments:
- humidity: bfloat16 [64, 128, 2560], P('lev', 'lat'), may hold values from -6 to 6
- wind_east: bfloat16 [64, 128, 2560], P('lev', 'lat'), may hold values from -6 to 6
- wind_north: bfloat16 [64, 128, 2560], P('lev', 'lat'), may hold values from -6 to 6
- legendre: bfloat16 [640, 640, 128], P('lat'), may hold values from -0.5 to 0.5
- owner: int32 [640], replicated, may hold values from 0 to 63, as said below
- vertical_modes: float32 [64, 64], replicated, may hold values from -1 to 1, as said below
- mode_values: float32 [64], replicated, may hold values from 0.2 to 2
Outputs:
- spectral: float32 [640, 640, 384], P('lat', 'lev')
Inputs may be any that keep to these rules, and one draw needn't show every extreme that they name: Every owner is named by exactly 10 wavenumbers, and wavenumbers m and 639 - m have the same owner. `vertical_modes`: an orthogonal matrix.
All inputs are finite; a program needn't handle non-finite values.
Results may differ from a plain program's by a relative error of at most 0.0048.
Values may be sent and summed in bfloat16 or wider, within the bound.
A program may use at most 64 MiB of HBM per device.

v0:
```python
import math

import jax
import jax.numpy as jnp
from jax import lax
from jax.sharding import PartitionSpec as P


def make_twiddle(waves, lon_count):
    longitude = jnp.arange(lon_count, dtype=jnp.int32)
    phase = waves[:, None] * longitude[None, :] % lon_count
    angle = phase.astype(jnp.float32) * (2.0 * math.pi / lon_count)
    factor = 1.0 / math.sqrt(lon_count)
    table = jnp.stack([jnp.cos(angle) * factor, -jnp.sin(angle) * factor], axis=1).astype(
        jnp.bfloat16
    )
    return table.reshape(-1, lon_count)


def project(table_rows, fourier):
    slot_count, parts, fields, levels, latitudes = fourier.shape
    flat = fourier.reshape(slot_count, parts * fields * levels, latitudes)
    result = jnp.einsum("snk,syk->sny", table_rows, flat, preferred_element_type=jnp.float32)
    return result.reshape(slot_count, table_rows.shape[1], parts, fields, levels)


def body(humidity, wind_east, wind_north, legendre, owner, vertical_modes, mode_values):
    trunc_count = owner.shape[0]
    slot_count = legendre.shape[0]
    level_count = vertical_modes.shape[0]
    lon_count = humidity.shape[2]
    row_block = trunc_count // lax.axis_size("lev")
    waves = jnp.arange(trunc_count, dtype=jnp.int32)
    order = jnp.argsort(owner * trunc_count + waves, stable=True)
    own_waves = lax.dynamic_slice_in_dim(order, lax.axis_index("lat") * slot_count, slot_count)
    twiddle = make_twiddle(order, lon_count)
    flux_east = (wind_east.astype(jnp.float32) * humidity.astype(jnp.float32)).astype(jnp.bfloat16)
    flux_north = (wind_north.astype(jnp.float32) * humidity.astype(jnp.float32)).astype(
        jnp.bfloat16
    )
    grid_rows = jnp.stack([humidity, flux_east, flux_north]).reshape(-1, lon_count)
    fourier = lax.dot_general(
        twiddle, grid_rows, (((1,), (1,)), ((), ())), preferred_element_type=jnp.float32
    )
    fourier = fourier.astype(jnp.bfloat16).reshape(
        trunc_count, 2, 3, humidity.shape[0], humidity.shape[1]
    )
    group_index = lax.axis_index("lev")
    block_waves = group_index * row_block + jnp.arange(row_block, dtype=jnp.int32)
    degree = block_waves.astype(jnp.float32)
    shift = 4.0 * degree * (degree + 1.0) / (trunc_count * trunc_count)
    inverse = 1.0 / (1.0 + shift[:, None] * mode_values[None, :])
    table_rows = lax.dynamic_slice_in_dim(legendre, group_index * row_block, row_block, 1)
    live = block_waves[None, :, None] >= own_waves[:, None, None]
    table_rows = jnp.where(live, table_rows, jnp.zeros_like(table_rows))
    owned = lax.all_to_all(fourier, "lat", split_axis=0, concat_axis=4, tiled=True)
    projected = project(table_rows, lax.all_gather(owned, "lev", axis=3, tiled=True))
    item_count = projected.shape[0]
    right = projected.reshape(item_count, row_block, 6, level_count)
    modal = jnp.einsum("inyj,jk->inyk", right, vertical_modes, precision=lax.Precision.HIGHEST)
    modal = modal * inverse[None, :, None, :]
    solved = jnp.einsum("inyk,lk->inyl", modal, vertical_modes, precision=lax.Precision.HIGHEST)
    return solved.reshape(item_count, row_block, 6 * level_count)


def solution(mesh):
    return jax.shard_map(
        body,
        mesh=mesh,
        in_specs=(
            P("lev", "lat", None),
            P("lev", "lat", None),
            P("lev", "lat", None),
            P("lat", None, None),
            P(),
            P(),
            P(),
        ),
        out_specs=P("lat", "lev", None),
        check_vma=False,
    )
```

profile of v0, /device:TPU:1, one launch (start us, length us, event | category | flops | bytes accessed | tf_op | source)
XLA Modules:
  0.0 259.8 jit_solution(15110283925857775987)
XLA Ops:
  0.0 0.0 copy-start
  0.0 0.7 iota_add_fusion
  0.7 4.4 %sort.17 = (s32[640]{0:T(1024)}, s32[640]{0:T(1024)S(1)}) sort(s32[640]{0:T(1024)S(1)} %iota_add_fusion, s32[640]{0:T(1024)S(1)} %iota.25), dimensions={0}, to_apply=%region_0.0 | sort | flops 6400 | bytes 10240 | tf_op jit(solution)/shard_map/jit(argsort)/sort | solution.py:34
  5.1 28.4 %multiply_convert_fusion.1 = (bf16[640,1,2560]{2,0,1:T(8,128)(2,1)S(1)}, bf16[640,1,2560]{2,0,1:T(8,128)(2,1)S(1)}) fusion(s32[640]{0:T(1024)S(1)} %get-tuple-element.6), kind=kLoop, calls=%fused_computation.5 | loop fusion | flops 22937600 | bytes 6556160 | tf_op jit(solution)/shard_map/convert
  33.5 0.6 pad_maximum_fusion
  34.1 29.4 %copy.25 = bf16[640,2,2560]{2,1,0:T(2,128)(2,1)} copy(bf16[640,2,2560]{2,0,1:T(8,128)(2,1)S(1)} %pad_maximum_fusion) | data formatting | bytes 13107200 | tf_op jit(solution)/shard_map/stack | solution.py:14
  63.5 0.0 copy-start.1
  63.5 0.0 copy-start.2
  63.5 0.0 copy-start.3
  63.5 14.2 %convert_element_type.52 = bf16[1280,2560]{1,0:T(8,128)(2,1)} reshape(bf16[640,2,2560]{2,1,0:T(2,128)(2,1)} %copy.25) | data formatting | bytes 13107200 | tf_op jit(solution)/shard_map/convert_element_type | solution.py:14
  77.8 0.0 copy-done.1
  77.8 0.0 copy-done.2
  77.8 0.0 copy-done.3
  77.8 0.1 fusion.14
  77.9 0.2 pad_maximum_fusion.1
  78.1 4.6 %convolution_convert_fusion = bf16[1280,24]{0,1:T(8,128)(2,1)S(1)} fusion(bf16[1280,2560]{1,0:T(8,128)(2,1)} %convert_element_type.52, bf16[24,2560]{1,0:T(8,128)(2,1)S(1)} %reshape.180), kind=kOutput, calls=%fused_computation.10 | convolution fusion | flops 157317120 | bytes 6737920 | tf_op jit(solution)/shard_map/dot_general | solution.py:42
  82.8 9.2 %reshape.181 = bf16[640,2,3,4,2]{1,0,4,3,2:T(8,128)(2,1)} reshape(bf16[1280,24]{0,1:T(8,128)(2,1)S(1)} %convolution_convert_fusion) | data formatting | bytes 122880 | tf_op jit(solution)/shard_map/reshape | solution.py:45
  91.9 0.0 copy-start.4
  91.9 24.7 %copy.26 = bf16[640,2,3,4,2]{3,4,2,1,0:T(2,128)(2,1)S(1)} copy(bf16[640,2,3,4,2]{1,0,4,3,2:T(8,128)(2,1)} %reshape.181) | data formatting | bytes 122880 | tf_op jit(solution)/shard_map/reshape | solution.py:45
  116.6 2.6 reshape.185
  119.2 23.1 %all-to-all-start = ((bf16[64,2,240]{2,1,0:T(2,128)(2,1)}), bf16[64,2,240]{2,1,0:T(2,128)(2,1)S(1)}, u32[]{:S(2)}, u32[]{:S(2)}) async-start(bf16[64,2,240]{2,1,0:T(2,128)(2,1)} %reshape.185), calls=%async_computation | async-start | bytes 131072 | tf_op jit(solution)/shard_map/all_to_all | solution.py:56
  142.4 0.1 dynamic_slice.6
  142.5 0.0 copy-done.4
  142.5 0.1 add_divide_fusion
  142.5 0.1 broadcast_compare_fusion
  142.6 10.9 %all-to-all-done = bf16[64,2,240]{2,1,0:T(2,128)(2,1)S(1)} async-done(((bf16[64,2,240]{2,1,0:T(2,128)(2,1)}), bf16[64,2,240]{2,1,0:T(2,128)(2,1)S(1)}, u32[]{:S(2)}, u32[]{:S(2)}) %all-to-all-start) | async-done | bytes 61472 | tf_op jit(solution)/shard_map/all_to_all | solution.py:56
  153.5 0.9 reshape.186
  154.3 7.7 %copy.33 = bf16[64,10,2,3,4,2]{1,0,5,4,3,2:T(8,128)(2,1)S(1)} copy(bf16[64,10,2,3,4,2]{4,5,3,2,1,0:T(2,128)(2,1)S(1)} %bitcast.25) | data formatting | bytes 122880 | tf_op jit(solution)/shard_map/all_to_all | solution.py:56
  162.0 0.8 copy.28
  162.9 80.6 %all_gather.3 = bf16[10,2,3,64,128]{0,4,3,2,1:T(8,128)(2,1)} all-gather(bf16[10,2,3,4,128]{0,4,3,2,1:T(8,128)(2,1)S(1)} %bitcast.27), channel_id=1, replica_groups=mesh['lev'=16,'lat'=64] {'lev'}, dimensions={3}, use_global_device_ids=true | all-gather | bytes 1044480 | tf_op jit(solution)/shard_map/all_gather | solution.py:57
  243.4 10.6 %copy.29 = bf16[10,2,3,64,128]{4,3,2,1,0:T(8,128)(2,1)S(1)} copy(bf16[10,2,3,64,128]{0,4,3,2,1:T(8,128)(2,1)} %all_gather.3) | data formatting | bytes 1966080 | tf_op jit(solution)/shard_map/all_gather | solution.py:57
  254.0 1.6 fusion.6
  255.6 0.4 reshape_reshape.3
  256.0 0.0 copy-done
  256.0 1.1 convolution_multiply_fusion
  257.1 1.1 fusion.15
  258.2 0.3 copy.31
  258.6 1.2 reshape.183
  (4 shorter events, 0.1 us)
Async XLA Ops:
  0.0 256.0 %copy-start = (f32[64,64]{1,0:T(8,128)S(1)}, f32[64,64]{1,0:T(8,128)}, u32[]{:S(2)}) copy-start(f32[64,64]{1,0:T(8,128)} %param.12) | copy-start | bytes 49156
  63.5 14.2 %copy-start.1 = (bf16[4,2,2560]{2,1,0:T(2,128)(2,1)S(1)}, bf16[4,2,2560]{2,1,0:T(2,128)(2,1)}, u32[]{:S(2)}) copy-start(bf16[4,2,2560]{2,1,0:T(2,128)(2,1)} %param.7) | copy-start | bytes 122884
  63.5 14.2 %copy-start.2 = (bf16[4,2,2560]{2,1,0:T(2,128)(2,1)S(1)}, bf16[4,2,2560]{2,1,0:T(2,128)(2,1)}, u32[]{:S(2)}) copy-start(bf16[4,2,2560]{2,1,0:T(2,128)(2,1)} %param.8) | copy-start | bytes 122884
  63.5 14.2 %copy-start.3 = (bf16[4,2,2560]{2,1,0:T(2,128)(2,1)S(1)}, bf16[4,2,2560]{2,1,0:T(2,128)(2,1)}, u32[]{:S(2)}) copy-start(bf16[4,2,2560]{2,1,0:T(2,128)(2,1)} %param.9) | copy-start | bytes 122884
  91.9 50.5 %copy-start.4 = (f32[64]{0:T(128)S(1)}, f32[64]{0:T(128)}, u32[]{:S(2)}) copy-start(f32[64]{0:T(128)} %param.13) | copy-start | bytes 772
  119.2 34.3 %all-to-all-start = ((bf16[64,2,240]{2,1,0:T(2,128)(2,1)}), bf16[64,2,240]{2,1,0:T(2,128)(2,1)S(1)}, u32[]{:S(2)}, u32[]{:S(2)}) async-start(bf16[64,2,240]{2,1,0:T(2,128)(2,1)} %reshape.185), calls=%async_computation | async-start | bytes 131072 | tf_op jit(solution)/shard_map/all_to_all | solution.py:56
where the time goes:
time: 261 us; the launch traced here: 260 us
  local copies, waits for them, and re-layouts  102 us (39%)
  blocking collectives  80.6 us (31%)
  other arithmetic  34.5 us (13%)
  starting transfers between devices  23.1 us (9%)
  waiting for transfers between devices  10.9 us (4%)
  matrix products  8.48 us (3%)
    all_gather x1, blocking collectives, body(): lax.all_gather(owned, 'lev', axis=3, tiled=True)  80.6 us
    reshape x2, local copies, waits for them, and re-layouts, body(): fourier.astype(jnp.bfloat16)  33.8 us
    another operation x1, local copies, waits for them, and re-layouts, make_twiddle(): jnp.stack([jnp.cos(angle) * factor, -jnp.sin(angle) * factor], axis=1)  29.4 us
    another operation x1, other arithmetic  28.4 us
    all_to_all x1, starting transfers between devices, body(): lax.all_to_all(fourier, 'lat', split_axis=0, concat_axis=4, tiled=True)  23.1 us
    convert_element_type x1, local copies, waits for them, and re-layouts, make_twiddle(): jnp.stack([jnp.cos(angle) * factor, -jnp.sin(angle) * factor], axis=1)  14.2 us
    all_to_all x1, waiting for transfers between devices, body(): lax.all_to_all(fourier, 'lat', split_axis=0, concat_axis=4, tiled=True)  10.9 us
    all_gather x1, local copies, waits for them, and re-layouts, body(): lax.all_gather(owned, 'lev', axis=3, tiled=True)  10.6 us
  transfers between devices with their start and end apart: 1, of which 1 were waited for; matrix products, arithmetic and copies ran while one was open for 0% of the time, Pallas kernels for 0%

commit v1 on v0

v1 whole, which is shorter than its diff:
```python
import functools
import math

import jax
import jax.numpy as jnp
import numpy as np
from jax import lax
from jax.experimental import pallas as pl
from jax.experimental.pallas import tpu as pltpu
from jax.sharding import PartitionSpec as P

MESH = pl.DeviceIdType.MESH
F32, BF16 = jnp.float32, jnp.bfloat16
RADIX = 20
CORES = 2


def split_lat(count):
    side = 1 << (int(math.log2(count)) // 2)
    return count // side, side


def lane_waves(units):
    rows = []
    for c in range(RADIX // 2):
        first, second = (0, RADIX // 2) if c == 0 else (c, RADIX - c)
        rows += [RADIX * u + first for u in range(units)] + [RADIX * u + second for u in range(units)]
    return np.array(rows)


def fourier_table(lon, units):
    inner = lon // RADIX
    waves = lane_waves(units).reshape(RADIX // 4, 4 * units)
    flip = np.ones((RADIX // 2, 2, units))
    flip[1:, 1] = -1.0
    flip = flip.reshape(RADIX // 4, 4 * units)
    phase = waves[:, None, :] * np.arange(inner)[None, :, None] % lon
    cos = np.cos(2 * np.pi * phase / lon) / math.sqrt(lon)
    sin = np.sin(2 * np.pi * phase / lon) / math.sqrt(lon)
    flip = flip[:, None, :]
    top = np.concatenate([cos, -sin], axis=2)
    bottom = np.concatenate([sin * flip, cos * flip], axis=2)
    return np.concatenate([top, bottom], axis=1)


def dot(a, b, contract=(1, 0)):
    return lax.dot_general(
        a, b, (((contract[0],), (contract[1],)), ((), ())), preferred_element_type=F32
    )


def iota(shape, axis):
    return lax.broadcasted_iota(jnp.int32, shape, axis)


def floor_div(value, divisor):
    return jnp.floor((value.astype(F32) + 0.5) * (1.0 / divisor))


def one_hot(mask):
    return jnp.where(mask, 1.0, 0.0).astype(BF16)


def short_fourier(x, inner):
    part = [x[:, inner * h : inner * (h + 1)] for h in range(RADIX)]
    half = RADIX // 2
    even = [part[h] + part[RADIX - h] for h in range(1, half)]
    odd = [part[h] - part[RADIX - h] for h in range(1, half)]
    real, imag = [None] * (half + 1), [None] * (half + 1)
    for q in range(half // 2 + 1):
        sums = []
        for parity in (0, 1):
            total = None
            for h in range(1, half):
                if h % 2 == parity:
                    factor = math.cos(2 * math.pi * ((q * h) % RADIX) / RADIX)
                    term = even[h - 1] * factor
                    total = term if total is None else total + term
            sums.append(total)
        ends_plus, ends_minus = part[0] + part[half], part[0] - part[half]
        first = sums[0] + (ends_plus if q % 2 == 0 else ends_minus)
        real[q] = first + sums[1]
        if q != half - q:
            other = sums[0] + (ends_plus if (half - q) % 2 == 0 else ends_minus)
            real[half - q] = other - sums[1]
    for q in range(half // 2 + 1):
        sums = []
        for parity in (0, 1):
            total = None
            for h in range(1, half):
                if h % 2 == parity:
                    factor = -math.sin(2 * math.pi * ((q * h) % RADIX) / RADIX)
                    term = odd[h - 1] * factor
                    total = term if total is None else total + term
            sums.append(total)
        imag[q] = sums[0] + sums[1]
        if q != half - q:
            imag[half - q] = sums[1] - sums[0]
    return real, imag


def kernel(
    cfg, hum_ref, east_ref, north_ref, leg_ref, owner_ref, modes_ref, values_ref, table_ref,
    out_ref,
    out_buf, x_buf, z_send, z_buf, y_buf, leg_raw, leg_buf, first_buf, last_buf, scale_buf, proj_buf,
    leg_sem, x_send, x_recv, z_send_sem, z_recv, up_send, up_recv, down_send, down_recv,
    side_send, side_recv,
):
    nx, nz, ny, slots, levels, trunc, lon, block = (
        cfg[k] for k in ("nx", "nz", "ny", "slots", "levels", "trunc", "lon", "block")
    )
    lev, lat = lax.axis_index("lev"), lax.axis_index("lat")
    x, z = lat // nz, lat % nz
    y, core = lev // CORES, lev % CORES
    inner, units = lon // RADIX, trunc // RADIX
    fields = 3
    piece = 2 * fields * levels
    rows = slots * piece
    width = out_buf.shape[1]
    lats = nx * nz * 2
    total_levels = ny * CORES * levels
    flat = 2 * fields * total_levels
    bundle = 2 * nz
    bundle_z = 2 * nx

    def along_x(i):
        return {"lat": ((x + i) % nx) * nz + z}

    def along_z(i):
        return {"lat": x * nz + (z + i) % nz}

    def along_y(i):
        return {"lev": ((y + i) % ny) * CORES + core}

    partner = {"lev": y * CORES + 1 - core}

    barrier = pltpu.get_barrier_semaphore()
    peers = [along_x(i) for i in range(1, nx)] + [along_z(i) for i in range(1, nz)]
    peers += [along_y(1), along_y(ny - 1), partner]
    for peer in peers:
        pl.semaphore_signal(barrier, inc=1, device_id=peer, device_id_type=MESH)

    leg_copy = pltpu.make_async_copy(
        leg_ref.at[:, pl.ds(pl.multiple_of(lev * block, 8), block), :], leg_raw, leg_sem
    )
    leg_copy.start()

    owner = owner_ref[...].astype(F32)
    owners = nx * nz
    member = owner == iota((owners, trunc), 0).astype(F32)
    before = one_hot(iota((trunc, trunc), 0) < iota((trunc, trunc), 1))
    count = dot(one_hot(member), before)
    rank = jnp.sum(jnp.where(member, count, 0.0), axis=0, keepdims=True)
    mine = (owner == lat.astype(F32)) & (rank == iota((16, trunc), 0).astype(F32))
    own_waves = jnp.sum(
        jnp.where(mine, iota((16, trunc), 1).astype(F32), 0.0), axis=1, keepdims=True
    )
    lane = iota((1, trunc), 1)
    clas = floor_div(lane, 2 * units)
    within = lane.astype(F32) - clas * (2 * units)
    second = within >= units
    unit = jnp.where(second, within - units, within)
    residue = jnp.where(second, jnp.where(clas == 0, RADIX // 2, RADIX - clas), clas)
    wave = RADIX * unit + residue
    reorder = one_hot(iota((trunc, trunc), 0).astype(F32) == wave)
    both = jnp.where(iota((16, trunc), 0) == 0, owner, jnp.where(iota((16, trunc), 0) == 1, rank, 0.0))
    both = dot(both.astype(BF16), reorder)
    owner_lane, rank_lane = both[0:1], both[1:2]

    humidity = hum_ref[...].astype(F32).reshape(2 * levels, lon)
    east = east_ref[...].astype(F32).reshape(2 * levels, lon)
    north = north_ref[...].astype(F32).reshape(2 * levels, lon)
    east = (east * humidity).astype(BF16).astype(F32)
    north = (north * humidity).astype(BF16).astype(F32)
    grid = jnp.concatenate([humidity, east, north], axis=0)
    real, imag = short_fourier(grid, inner)
    joined = [jnp.concatenate([r, i], axis=1) for r, i in zip(real, imag)]
    grid_rows = grid.shape[0]
    reals, imags = [], []
    for p in range(RADIX // 4):
        table = table_ref[p]
        if p == 0:
            left = jnp.concatenate([joined[0], joined[RADIX // 2], joined[1]], axis=0)
            limits = [units, 2 * units]
        else:
            left = jnp.concatenate([joined[2 * p], joined[2 * p + 1]], axis=0)
            limits = [2 * units]
        high = left.astype(BF16)
        low = (left - high.astype(F32)).astype(BF16)
        result = dot(high, table) + dot(low, table) + dot(high, table_ref[RADIX // 4 + p])
        column = iota((grid_rows, 8 * units), 1)
        column = jnp.where(column >= 4 * units, column - 4 * units, column)
        picked = result[len(limits) * grid_rows :]
        for k in reversed(range(len(limits))):
            picked = jnp.where(
                column < limits[k], result[k * grid_rows : (k + 1) * grid_rows], picked
            )
        reals.append(picked[:, : 4 * units])
        imags.append(picked[:, 4 * units :])
    spectrum = jnp.concatenate(
        [jnp.concatenate(reals, axis=1), jnp.concatenate(imags, axis=1)], axis=0
    ).astype(BF16)

    source = iota((piece, 2 * grid_rows), 1)
    target = iota((piece, 2 * grid_rows), 0)
    spread = []
    for t in range(2):
        pick = one_hot(2 * target + t == source)
        spread.append(dot(pick, spectrum))
    halves = []
    for t in range(2):
        pieces = [
            jnp.where(rank_lane == float(s), spread[t], 0.0) for s in range(slots)
        ] + [jnp.zeros((width - rows, trunc), F32)]
        halves.append(jnp.concatenate(pieces, axis=0))
    right = jnp.concatenate(halves, axis=1).astype(BF16)
    row = iota((2 * owners, trunc), 0).astype(F32)
    choose = jnp.concatenate(
        [
            jnp.where(2.0 * owner_lane == row, 1.0, 0.0),
            jnp.where(2.0 * owner_lane + 1.0 == row, 1.0, 0.0),
        ],
        axis=1,
    ).astype(BF16)
    out_buf[...] = dot(choose, right, (1, 1)).astype(BF16)

    pl.semaphore_wait(barrier, len(peers))

    copies = []
    for i in range(1, nx):
        to = (x + i) % nx
        copy = pltpu.make_async_remote_copy(
            src_ref=out_buf.at[pl.ds(pl.multiple_of(to * bundle, bundle), bundle)],
            dst_ref=x_buf.at[pl.ds(pl.multiple_of(x * bundle, bundle), bundle)],
            send_sem=x_send.at[i],
            recv_sem=x_recv.at[i],
            device_id=along_x(i),
            device_id_type=MESH,
        )
        copy.start()
        copies.append(copy)
    x_buf[pl.ds(pl.multiple_of(x * bundle, bundle), bundle), :] = out_buf[
        pl.ds(pl.multiple_of(x * bundle, bundle), bundle), :
    ]

    leg_copy.wait()
    arrive = iota((lats, lats), 1)
    from_z = arrive // bundle_z
    from_x = (arrive % bundle_z) // 2
    reach = one_hot(iota((lats, lats), 0) == (from_x * nz + from_z) * 2 + arrive % 2)
    leg = leg_raw[...].astype(F32).reshape(slots * block, lats).astype(BF16)
    leg = dot(leg, reach)
    degree = iota((block, lats), 0).astype(F32) + (lev * block).astype(F32)
    for s in range(slots):
        live = degree >= own_waves[s : s + 1, :]
        leg_buf[block * s : block * (s + 1), :] = jnp.where(
            live, leg[block * s : block * (s + 1)], 0.0
        )

    swap_to = iota((2 * owners, 2 * owners), 0)
    swap_from = iota((2 * owners, 2 * owners), 1)
    part_z, part_x, part_t = swap_to // bundle_z, (swap_to % bundle_z) // 2, swap_to % 2
    swap = one_hot(swap_from == part_x * bundle + part_z * 2 + part_t)

    for copy in copies:
        copy.wait_recv()
    z_send[...] = dot(swap, x_buf[...]).astype(BF16)
    copies_z = []
    for i in range(1, nz):
        to = (z + i) % nz
        copy = pltpu.make_async_remote_copy(
            src_ref=z_send.at[pl.ds(pl.multiple_of(to * bundle_z, bundle_z), bundle_z)],
            dst_ref=z_buf.at[pl.ds(pl.multiple_of(z * bundle_z, bundle_z), bundle_z)],
            send_sem=z_send_sem.at[i],
            recv_sem=z_recv.at[i],
            device_id=along_z(i),
            device_id_type=MESH,
        )
        copy.start()
        copies_z.append(copy)
    z_buf[pl.ds(pl.multiple_of(z * bundle_z, bundle_z), bundle_z), :] = z_send[
        pl.ds(pl.multiple_of(z * bundle_z, bundle_z), bundle_z), :
    ]

    modes = modes_ref[...]
    modes_high = modes.astype(BF16)
    modes_low = (modes - modes_high.astype(F32)).astype(BF16)
    tl = total_levels
    tile = one_hot(iota((tl, flat), 0) == (iota((tl, flat), 1) & (tl - 1)))
    column_part = iota((flat, flat), 1) // tl
    row_id = iota((flat, flat), 0)
    group = floor_div(row_id, piece)
    row_in = row_id.astype(F32) - group * piece
    row_part = floor_div(row_in, levels)
    id64 = iota((flat, tl), 0)
    group64 = floor_div(id64, piece)
    level64 = id64.astype(F32) - group64 * piece
    level64 = level64 - floor_div(level64, levels) * levels + levels * group64
    gather = one_hot(level64 == iota((flat, tl), 1).astype(F32))
    for k, part in enumerate((modes_high, modes_low)):
        wide = dot(part, tile).astype(BF16)
        first_buf[k] = jnp.where(
            row_part == column_part.astype(F32), dot(gather, wide), 0.0
        ).astype(BF16)
        tall = dot(tile, part, (0, 1)).astype(BF16)
        last_buf[k] = jnp.where(row_id // tl == column_part, dot(tall, tile), 0.0).astype(BF16)
    values = jnp.concatenate([values_ref[...]] * (2 * fields), axis=1)
    number = iota((block, flat), 0).astype(F32) + (lev * block).astype(F32)
    shift = 4.0 * number * (number + 1.0) / (trunc * trunc)
    scale_buf[...] = 1.0 / (1.0 + shift * values)

    for copy in copies_z:
        copy.wait_recv()
    own = z_buf[...].astype(F32).T
    y_buf[lev] = own[:rows].astype(BF16)

    chunks = cfg["chunks"]
    starts = [sum(chunks[:k]) for k in range(len(chunks))]
    half = len(chunks) // 2
    far = ny // 2
    pending = []

    def send(group_id, k, send_sem, recv_sem, to):
        view = y_buf.at[group_id, pl.ds(starts[k], chunks[k])]
        copy = pltpu.make_async_remote_copy(
            src_ref=view, dst_ref=view, send_sem=send_sem, recv_sem=recv_sem,
            device_id=to, device_id_type=MESH,
        )
        copy.start()
        pending.append(copy)

    def arrival(group_id, k, sem):
        view = y_buf.at[group_id, pl.ds(starts[k], chunks[k])]
        pltpu.make_async_remote_copy(
            src_ref=view, dst_ref=view, send_sem=sem, recv_sem=sem,
            device_id=partner, device_id_type=MESH,
        ).wait_recv()

    for k in range(len(chunks)):
        send(lev, k, up_send.at[0, k], up_recv.at[0, k], along_y(1))
        send(lev, k, down_send.at[0, k], down_recv.at[0, k], along_y(ny - 1))
    for k in range(len(chunks)):
        send(lev, k, side_send.at[0, k], side_recv.at[0, k], partner)
    for d in range(1, far + 1):
        below = ((y + ny - d) % ny) * CORES + core
        above = ((y + d) % ny) * CORES + core
        for k in range(len(chunks)):
            if d < far or k < half:
                arrival(below, k, up_recv.at[d - 1, k])
                if d < far - 1 or (d == far - 1 and k < half):
                    send(below, k, up_send.at[d, k], up_recv.at[d, k], along_y(1))
                send(below, k, side_send.at[d, k], side_recv.at[d, k], partner)
            if d < far or k >= half:
                arrival(above, k, down_recv.at[d - 1, k])
                if d < far - 1 or (d == far - 1 and k >= half):
                    send(above, k, down_send.at[d, k], down_recv.at[d, k], along_y(ny - 1))
                if d < far:
                    send(above, k, side_send.at[far + d, k], side_recv.at[far + d, k], partner)
                else:
                    send(above, k, side_send.at[d, k], side_recv.at[d, k], partner)
    other = 1 - core
    for d in range(far + 1):
        for k in range(len(chunks)):
            arrival(((y + ny - d) % ny) * CORES + other, k, side_recv.at[d, k])
            if 0 < d < far:
                arrival(((y + d) % ny) * CORES + other, k, side_recv.at[far + d, k])

    for s in range(slots):
        right = jnp.concatenate(
            [y_buf[g, piece * s : piece * (s + 1), :] for g in range(ny * CORES)], axis=0
        )
        left = leg_buf[block * s : block * (s + 1), :].astype(BF16)
        proj_buf[block * s : block * (s + 1), :] = dot(left, right, (1, 1))
    projected = proj_buf[...].astype(BF16)
    modal = dot(projected, first_buf[0]) + dot(projected, first_buf[1])
    scale = jnp.concatenate([scale_buf[...]] * slots, axis=0)
    modal = (modal * scale).astype(BF16)
    solved = dot(modal, last_buf[0]) + dot(modal, last_buf[1])
    out_ref[...] = solved.reshape(slots, block, flat)

    for copy in copies + copies_z + pending:
        copy.wait_send()


def build(nx, nz, ny, slots, levels, trunc, lon, chunks, width):
    block = trunc // (ny * CORES)
    rows = slots * 6 * levels
    flat = 6 * levels * ny * CORES
    lats = nx * nz * 2
    far = ny // 2
    cfg = dict(
        nx=nx, nz=nz, ny=ny, slots=slots, levels=levels, trunc=trunc, lon=lon, block=block,
        chunks=chunks,
    )
    dma = pltpu.SemaphoreType.DMA
    vmem = pl.BlockSpec(memory_space=pltpu.VMEM)
    hbm = pl.BlockSpec(memory_space=pl.ANY)
    nc = len(chunks)
    return pl.pallas_call(
        functools.partial(kernel, cfg),
        out_shape=jax.ShapeDtypeStruct((slots, block, flat), F32),
        in_specs=[vmem, vmem, vmem, hbm, vmem, vmem, vmem, vmem],
        out_specs=vmem,
        scratch_shapes=[
            pltpu.VMEM((lats, width), BF16),
            pltpu.VMEM((lats, width), BF16),
            pltpu.VMEM((lats, width), BF16),
            pltpu.VMEM((lats, width), BF16),
            pltpu.VMEM((ny * CORES, rows, lats), BF16),
            pltpu.VMEM((slots, block, lats), BF16),
            pltpu.VMEM((slots * block, lats), F32),
            pltpu.VMEM((2, flat, flat), BF16),
            pltpu.VMEM((2, flat, flat), BF16),
            pltpu.VMEM((block, flat), F32),
            pltpu.VMEM((slots * block, flat), F32),
            dma, dma((nx,)), dma((nx,)), dma((nz,)), dma((nz,)),
            dma((far, nc)), dma((far, nc)), dma((far, nc)), dma((far, nc)),
            dma((ny, nc)), dma((ny, nc)),
        ],
        compiler_params=pltpu.CompilerParams(
            collective_id=0, has_side_effects=True, vmem_limit_bytes=60 * 1024 * 1024
        ),
    )


def body(humidity, wind_east, wind_north, legendre, owner, vertical_modes, mode_values):
    trunc = owner.shape[0]
    levels, pair, lon = humidity.shape
    owners = lax.axis_size("lat")
    nx, nz = split_lat(owners)
    ny = lax.axis_size("lev") // CORES
    slots = legendre.shape[0]
    rows = slots * 6 * levels
    if rows % 16 == 0 and rows >= 64:
        quarter = -(-rows // 64) * 16
        chunks = [quarter] * 3 + [rows - 3 * quarter]
    else:
        chunks = [rows // 2, rows - rows // 2]
    width = -(-rows // 128) * 128
    table = fourier_table(lon, trunc // RADIX)
    high = table.astype(BF16)
    table = jnp.asarray(np.concatenate([high, (table - high.astype(np.float64)).astype(BF16)]))
    call = build(nx, nz, ny, slots, levels, trunc, lon, chunks, width)
    return call(
        humidity, wind_east, wind_north, legendre, owner.reshape(1, trunc), vertical_modes,
        mode_values.reshape(1, -1), table,
    )


def solution(mesh):
    return jax.shard_map(
        body,
        mesh=mesh,
        in_specs=(
            P("lev", "lat", None),
            P("lev", "lat", None),
            P("lev", "lat", None),
            P("lat", None, None),
            P(),
            P(),
            P(),
        ),
        out_specs=P("lat", "lev", None),
        check_vma=False,
    )
```

time: 261 us -> 56 us (0.21)
  local copies, waits for them, and re-layouts: 102 us -> 3.2 us
  blocking collectives: 80.6 us -> 0 us
  Pallas kernels: 0 us -> 52.6 us
  other arithmetic: 34.5 us -> 0 us
  starting transfers between devices: 23.1 us -> 0 us
  waiting for transfers between devices: 10.9 us -> 0 us
  matrix products: 8.48 us -> 0 us
    all_gather x1 -> x0, blocking collectives: 80.6 us -> none  [body(): lax.all_gather(owned, 'lev', axis=3, tiled=True)]
    pallas_call x0 -> x1, Pallas kernels: none -> 52.6 us  [body(): call(humidity, wind_east, wind_north, legendre, owner.reshape(1, trunc),...]
    reshape x4 -> x1, local copies, waits for them, and re-layouts: 35.1 us -> 1.27 us  [body(): owner.reshape(1, trunc)]
    another operation x2 -> x0, local copies, waits for them, and re-layouts: 29.8 us -> none  [the longest x1 29.4 us: make_twiddle(): jnp.stack([jnp.cos(angle) * factor, -jnp.sin(angle) * factor], axis=1)]
    another operation x4 -> x0, other arithmetic: 29.3 us -> none
    all_to_all x1 -> x0, starting transfers between devices: 23.1 us -> none  [body(): lax.all_to_all(fourier, 'lat', split_axis=0, concat_axis=4, tiled=True)]
    convert_element_type x1 -> x0, local copies, waits for them, and re-layouts: 14.2 us -> none  [make_twiddle(): jnp.stack([jnp.cos(angle) * factor, -jnp.sin(angle) * factor], axis=1)]
    all_to_all x1 -> x0, waiting for transfers between devices: 10.9 us -> none  [body(): lax.all_to_all(fourier, 'lat', split_axis=0, concat_axis=4, tiled=True)]
  transfers between devices with their start and end apart: 1 -> 0, of which waited for: 1 -> 0; matrix products, arithmetic and copies ran while one was open for 0% -> 0% of each run, Pallas kernels for 0% -> 0%
where the time goes in v1:
time: 56 us; the launch traced here: 55.8 us
  Pallas kernels  52.6 us (94%)
  local copies, waits for them, and re-layouts  3.2 us (6%)
    pallas_call x1, Pallas kernels, body(): call(humidity, wind_east, wind_north, legendre, owner.reshape(1, trunc),...  52.6 us
    unnamed x1, local copies, waits for them, and re-layouts  1.94 us
    reshape x1, local copies, waits for them, and re-layouts, body(): owner.reshape(1, trunc)  1.27 us

profile of v1, /device:TPU:1, one launch (start us, length us, event | category | flops | bytes accessed | tf_op | source)
XLA Modules:
  0.0 55.8 jit_solution(2420402896094687077)
XLA Ops:
  0.0 1.3 %reshape.6.owner_ref = s32[1,640]{1,0:T(1,128)} reshape(s32[640]{0:T(1024)} %param.12) | data formatting | bytes 5120 | tf_op jit(solution)/shard_map/reshape | solution.py:445
  1.3 52.6 %shard_map.82 = f32[10,40,384]{2,1,0:T(8,128)} custom-call(bf16[4,2,2560]{2,1,0:T(2,128)(2,1)} %hum_ref.1, bf16[4,2,2560]{2,1,0:T(2,128)(2,1)} %east_ref.1, bf16[4,2,2560]{2,1,0:T(2,128)(2,1)} %north_ref.1, bf16[10,640,128]{2,1,0:T(8,128)(2,1)} %leg_ref.1, s32[1,640]{1,0:T(1,128)} %reshape.6.owner_ref, f32[64,64]{1,0:T(8,128)} %modes_ref.1, ...), custom_call_target="tpu_custom_call" | custom-call | tf_op jit(solution)/shard_map/pallas_call | solution.py:444
  53.8 1.9 %copy.10 = f32[10,40,384]{2,1,0:T(8,128)} copy(f32[10,40,384]{2,1,0:T(8,128)} %shard_map.82) | data formatting | bytes 1228800

commit v2 on v1

--- a/solution.py
+++ b/solution.py
@@ -13,6 +13,7 @@
 F32, BF16 = jnp.float32, jnp.bfloat16
 RADIX = 20
 CORES = 2
+VMEM_LIMIT = 24 * 1024 * 1024
 
 
 def split_lat(count):
@@ -41,6 +42,11 @@
     top = np.concatenate([cos, -sin], axis=2)
     bottom = np.concatenate([sin * flip, cos * flip], axis=2)
     return np.concatenate([top, bottom], axis=1)
+
+
+def place(rel, side):
+    order = (0, 1, 7, 2, 6, 3, 5, 4).index(rel)
+    return side * 5 + order if order < 5 else 10 + side * 3 + order - 5
 
 
 def dot(a, b, contract=(1, 0)):
@@ -100,11 +106,12 @@
 
 
 def kernel(
-    cfg, hum_ref, east_ref, north_ref, leg_ref, owner_ref, modes_ref, values_ref, table_ref,
+    cfg, hum_hbm, east_hbm, north_hbm, leg_ref, owner_hbm, modes_hbm, values_hbm, table_hbm,
     out_ref,
-    out_buf, x_buf, z_send, z_buf, y_buf, leg_raw, leg_buf, first_buf, last_buf, scale_buf, proj_buf,
-    leg_sem, x_send, x_recv, z_send_sem, z_recv, up_send, up_recv, down_send, down_recv,
-    side_send, side_recv,
+    hum_ref, east_ref, north_ref, owner_ref, modes_ref, values_ref, table_ref,
+    out_buf, x_buf, z_send, z_buf, y_buf, leg_raw, leg_buf, first_buf, last_buf, scale_buf,
+    modal_buf,
+    load_sem, leg_sem, x_send, x_recv, z_send_sem, z_recv, y_send, y_recv,
 ):
     nx, nz, ny, slots, levels, trunc, lon, block = (
         cfg[k] for k in ("nx", "nz", "ny", "slots", "levels", "trunc", "lon", "block")
@@ -136,24 +143,33 @@
 
     barrier = pltpu.get_barrier_semaphore()
     peers = [along_x(i) for i in range(1, nx)] + [along_z(i) for i in range(1, nz)]
-    peers += [along_y(1), along_y(ny - 1), partner]
+    peers += [along_y(1), along_y(ny - 1), along_y(2), along_y(ny - 2), partner]
     for peer in peers:
         pl.semaphore_signal(barrier, inc=1, device_id=peer, device_id_type=MESH)
 
+    loads = []
+    for k, (source, target) in enumerate((
+        (owner_hbm, owner_ref), (hum_hbm, hum_ref), (east_hbm, east_ref), (north_hbm, north_ref),
+        (table_hbm, table_ref), (modes_hbm, modes_ref), (values_hbm, values_ref),
+    )):
+        loads.append(pltpu.make_async_copy(source, target, load_sem.at[k]))
+        loads[-1].start()
     leg_copy = pltpu.make_async_copy(
         leg_ref.at[:, pl.ds(pl.multiple_of(lev * block, 8), block), :], leg_raw, leg_sem
     )
     leg_copy.start()
 
-    owner = owner_ref[...].astype(F32)
+    loads[0].wait()
+    owner = owner_ref[...].reshape(1, trunc).astype(F32)
     owners = nx * nz
     member = owner == iota((owners, trunc), 0).astype(F32)
     before = one_hot(iota((trunc, trunc), 0) < iota((trunc, trunc), 1))
     count = dot(one_hot(member), before)
     rank = jnp.sum(jnp.where(member, count, 0.0), axis=0, keepdims=True)
-    mine = (owner == lat.astype(F32)) & (rank == iota((16, trunc), 0).astype(F32))
+    tall_slots = -(-slots // 8) * 8
+    mine = (owner == lat.astype(F32)) & (rank == iota((tall_slots, trunc), 0).astype(F32))
     own_waves = jnp.sum(
-        jnp.where(mine, iota((16, trunc), 1).astype(F32), 0.0), axis=1, keepdims=True
+        jnp.where(mine, iota((tall_slots, trunc), 1).astype(F32), 0.0), axis=1, keepdims=True
     )
     lane = iota((1, trunc), 1)
     clas = floor_div(lane, 2 * units)
@@ -167,6 +183,8 @@
     both = dot(both.astype(BF16), reorder)
     owner_lane, rank_lane = both[0:1], both[1:2]
 
+    for copy in loads[1:5]:
+        copy.wait()
     humidity = hum_ref[...].astype(F32).reshape(2 * levels, lon)
     east = east_ref[...].astype(F32).reshape(2 * levels, lon)
     north = north_ref[...].astype(F32).reshape(2 * levels, lon)
@@ -282,6 +300,8 @@
         pl.ds(pl.multiple_of(z * bundle_z, bundle_z), bundle_z), :
     ]
 
+    loads[5].wait()
+    loads[6].wait()
     modes = modes_ref[...]
     modes_high = modes.astype(BF16)
     modes_low = (modes - modes_high.astype(F32)).astype(BF16)
@@ -295,7 +315,14 @@
     id64 = iota((flat, tl), 0)
     group64 = floor_div(id64, piece)
     level64 = id64.astype(F32) - group64 * piece
-    level64 = level64 - floor_div(level64, levels) * levels + levels * group64
+    bases = [None] * (ny * CORES)
+    for rel in range(ny):
+        for side in range(CORES):
+            level_group = ((y + rel) % ny) * CORES + (core if side == 0 else 1 - core)
+            bases[place(rel, side)] = jnp.full(
+                (piece, tl), (level_group * levels).astype(F32), F32
+            )
+    level64 = level64 - floor_div(level64, levels) * levels + jnp.concatenate(bases, axis=0)
     gather = one_hot(level64 == iota((flat, tl), 1).astype(F32))
     for k, part in enumerate((modes_high, modes_low)):
         wide = dot(part, tile).astype(BF16)
@@ -304,7 +331,7 @@
         ).astype(BF16)
         tall = dot(tile, part, (0, 1)).astype(BF16)
         last_buf[k] = jnp.where(row_id // tl == column_part, dot(tall, tile), 0.0).astype(BF16)
-    values = jnp.concatenate([values_ref[...]] * (2 * fields), axis=1)
+    values = jnp.concatenate([values_ref[...].reshape(1, tl)] * (2 * fields), axis=1)
     number = iota((block, flat), 0).astype(F32) + (lev * block).astype(F32)
     shift = 4.0 * number * (number + 1.0) / (trunc * trunc)
     scale_buf[...] = 1.0 / (1.0 + shift * values)
@@ -312,67 +339,90 @@
     for copy in copies_z:
         copy.wait_recv()
     own = z_buf[...].astype(F32).T
-    y_buf[lev] = own[:rows].astype(BF16)
-
-    chunks = cfg["chunks"]
-    starts = [sum(chunks[:k]) for k in range(len(chunks))]
-    half = len(chunks) // 2
-    far = ny // 2
+    y_buf[place(0, 0)] = own[:rows].astype(BF16)
+
     pending = []
-
-    def send(group_id, k, send_sem, recv_sem, to):
-        view = y_buf.at[group_id, pl.ds(starts[k], chunks[k])]
-        copy = pltpu.make_async_remote_copy(
-            src_ref=view, dst_ref=view, send_sem=send_sem, recv_sem=recv_sem,
-            device_id=to, device_id_type=MESH,
+    half = cfg["half"]
+
+    def message(k, rel, to, to_rel, side, start=0, size=rows):
+        return pltpu.make_async_remote_copy(
+            src_ref=y_buf.at[place(rel, 0), pl.ds(start, size)],
+            dst_ref=y_buf.at[place(to_rel, side), pl.ds(start, size)],
+            send_sem=y_send.at[k],
+            recv_sem=y_recv.at[k],
+            device_id=to,
+            device_id_type=MESH,
         )
+
+    def send(k, rel, step, start=0, size=rows):
+        copy = message(k, rel, along_y(step % ny), (rel - step) % ny, 0, start, size)
         copy.start()
         pending.append(copy)
 
-    def arrival(group_id, k, sem):
-        view = y_buf.at[group_id, pl.ds(starts[k], chunks[k])]
+    def hand(k, rel):
+        copy = message(k, rel, partner, rel, 1)
+        copy.start()
+        pending.append(copy)
+
+    def arrive_from(k, rel, side, start=0, size=rows):
         pltpu.make_async_remote_copy(
-            src_ref=view, dst_ref=view, send_sem=sem, recv_sem=sem,
-            device_id=partner, device_id_type=MESH,
+            src_ref=y_buf.at[place(rel, side), pl.ds(start, size)],
+            dst_ref=y_buf.at[place(rel, side), pl.ds(start, size)],
+            send_sem=y_send.at[k],
+            recv_sem=y_recv.at[k],
+            device_id=partner,
+            device_id_type=MESH,
         ).wait_recv()
 
-    for k in range(len(chunks)):
-        send(lev, k, up_send.at[0, k], up_recv.at[0, k], along_y(1))
-        send(lev, k, down_send.at[0, k], down_recv.at[0, k], along_y(ny - 1))
-    for k in range(len(chunks)):
-        send(lev, k, side_send.at[0, k], side_recv.at[0, k], partner)
-    for d in range(1, far + 1):
-        below = ((y + ny - d) % ny) * CORES + core
-        above = ((y + d) % ny) * CORES + core
-        for k in range(len(chunks)):
-            if d < far or k < half:
-                arrival(below, k, up_recv.at[d - 1, k])
-                if d < far - 1 or (d == far - 1 and k < half):
-                    send(below, k, up_send.at[d, k], up_recv.at[d, k], along_y(1))
-                send(below, k, side_send.at[d, k], side_recv.at[d, k], partner)
-            if d < far or k >= half:
-                arrival(above, k, down_recv.at[d - 1, k])
-                if d < far - 1 or (d == far - 1 and k >= half):
-                    send(above, k, down_send.at[d, k], down_recv.at[d, k], along_y(ny - 1))
-                if d < far:
-                    send(above, k, side_send.at[far + d, k], side_recv.at[far + d, k], partner)
-                else:
-                    send(above, k, side_send.at[d, k], side_recv.at[d, k], partner)
-    other = 1 - core
-    for d in range(far + 1):
-        for k in range(len(chunks)):
-            arrival(((y + ny - d) % ny) * CORES + other, k, side_recv.at[d, k])
-            if 0 < d < far:
-                arrival(((y + d) % ny) * CORES + other, k, side_recv.at[far + d, k])
-
-    for s in range(slots):
-        right = jnp.concatenate(
-            [y_buf[g, piece * s : piece * (s + 1), :] for g in range(ny * CORES)], axis=0
-        )
-        left = leg_buf[block * s : block * (s + 1), :].astype(BF16)
-        proj_buf[block * s : block * (s + 1), :] = dot(left, right, (1, 1))
-    projected = proj_buf[...].astype(BF16)
-    modal = dot(projected, first_buf[0]) + dot(projected, first_buf[1])
+    send(0, 0, 2)
+    send(1, 0, -2)
+    send(2, 0, 1)
+    send(3, 0, -1)
+    hand(8, 0)
+    arrive_from(0, ny - 2, 0)
+    send(4, ny - 2, 2, 0, half)
+    send(5, ny - 2, 1)
+    arrive_from(1, 2, 0)
+    send(6, 2, -2, half, rows - half)
+    send(7, 2, -1)
+    hand(9, ny - 2)
+    hand(10, 2)
+    arrive_from(2, ny - 1, 0)
+    hand(11, ny - 1)
+    arrive_from(3, 1, 0)
+    hand(12, 1)
+    arrive_from(8, 0, 1)
+    arrive_from(9, ny - 2, 1)
+    arrive_from(10, 2, 1)
+    arrive_from(11, ny - 1, 1)
+    arrive_from(12, 1, 1)
+
+    def modal_part(first, last):
+        pieces = []
+        for s in range(slots):
+            right = jnp.concatenate(
+                [y_buf[g, piece * s : piece * (s + 1), :] for g in range(first, last)], axis=0
+            )
+            left = leg_buf[block * s : block * (s + 1), :].astype(BF16)
+            pieces.append(dot(left, right, (1, 1)))
+        projected = jnp.concatenate(pieces, axis=0).astype(BF16)
+        span = slice(first * piece, last * piece)
+        return dot(projected, first_buf[0, span, :]) + dot(projected, first_buf[1, span, :])
+
+    near, groups = 10, ny * CORES
+    modal_buf[...] = modal_part(0, near)
+    arrive_from(5, ny - 3, 0)
+    hand(13, ny - 3)
+    arrive_from(7, 3, 0)
+    hand(14, 3)
+    arrive_from(4, 4, 0, 0, half)
+    arrive_from(6, 4, 0, half, rows - half)
+    hand(15, 4)
+    modal_buf[...] += modal_part(near, near + 3)
+    arrive_from(13, ny - 3, 1)
+    arrive_from(14, 3, 1)
+    arrive_from(15, 4, 1)
+    modal = modal_buf[...] + modal_part(near + 3, groups)
     scale = jnp.concatenate([scale_buf[...]] * slots, axis=0)
     modal = (modal * scale).astype(BF16)
     solved = dot(modal, last_buf[0]) + dot(modal, last_buf[1])
@@ -382,26 +432,32 @@
         copy.wait_send()
 
 
-def build(nx, nz, ny, slots, levels, trunc, lon, chunks, width):
+def build(nx, nz, ny, slots, levels, trunc, lon, half, width):
     block = trunc // (ny * CORES)
     rows = slots * 6 * levels
-    flat = 6 * levels * ny * CORES
+    total_levels = levels * ny * CORES
+    flat = 6 * total_levels
     lats = nx * nz * 2
-    far = ny // 2
+    inner, units = lon // RADIX, trunc // RADIX
     cfg = dict(
         nx=nx, nz=nz, ny=ny, slots=slots, levels=levels, trunc=trunc, lon=lon, block=block,
-        chunks=chunks,
+        half=half,
     )
     dma = pltpu.SemaphoreType.DMA
-    vmem = pl.BlockSpec(memory_space=pltpu.VMEM)
-    hbm = pl.BlockSpec(memory_space=pl.ANY)
-    nc = len(chunks)
+    hbm = pl.BlockSpec(memory_space=pltpu.HBM)
     return pl.pallas_call(
         functools.partial(kernel, cfg),
         out_shape=jax.ShapeDtypeStruct((slots, block, flat), F32),
-        in_specs=[vmem, vmem, vmem, hbm, vmem, vmem, vmem, vmem],
-        out_specs=vmem,
+        in_specs=[hbm] * 8,
+        out_specs=pl.BlockSpec(memory_space=pltpu.VMEM),
         scratch_shapes=[
+            pltpu.VMEM((levels, 2, lon), BF16),
+            pltpu.VMEM((levels, 2, lon), BF16),
+            pltpu.VMEM((levels, 2, lon), BF16),
+            pltpu.VMEM((trunc,), jnp.int32),
+            pltpu.VMEM((total_levels, total_levels), F32),
+            pltpu.VMEM((total_levels,), F32),
+            pltpu.VMEM((RADIX // 2, 2 * inner, 8 * units), BF16),
             pltpu.VMEM((lats, width), BF16),
             pltpu.VMEM((lats, width), BF16),
             pltpu.VMEM((lats, width), BF16),
@@ -413,12 +469,10 @@
             pltpu.VMEM((2, flat, flat), BF16),
             pltpu.VMEM((block, flat), F32),
             pltpu.VMEM((slots * block, flat), F32),
-            dma, dma((nx,)), dma((nx,)), dma((nz,)), dma((nz,)),
-            dma((far, nc)), dma((far, nc)), dma((far, nc)), dma((far, nc)),
-            dma((ny, nc)), dma((ny, nc)),
+            dma((7,)), dma, dma((nx,)), dma((nx,)), dma((nz,)), dma((nz,)), dma((16,)), dma((16,)),
         ],
         compiler_params=pltpu.CompilerParams(
-            collective_id=0, has_side_effects=True, vmem_limit_bytes=60 * 1024 * 1024
+            collective_id=0, has_side_effects=True, vmem_limit_bytes=VMEM_LIMIT
         ),
     )
 
@@ -431,20 +485,14 @@
     ny = lax.axis_size("lev") // CORES
     slots = legendre.shape[0]
     rows = slots * 6 * levels
-    if rows % 16 == 0 and rows >= 64:
-        quarter = -(-rows // 64) * 16
-        chunks = [quarter] * 3 + [rows - 3 * quarter]
-    else:
-        chunks = [rows // 2, rows - rows // 2]
+    half = -(-rows // 32) * 16
     width = -(-rows // 128) * 128
     table = fourier_table(lon, trunc // RADIX)
     high = table.astype(BF16)
     table = jnp.asarray(np.concatenate([high, (table - high.astype(np.float64)).astype(BF16)]))
-    call = build(nx, nz, ny, slots, levels, trunc, lon, chunks, width)
-    return call(
-        humidity, wind_east, wind_north, legendre, owner.reshape(1, trunc), vertical_modes,
-        mode_values.reshape(1, -1), table,
-    )
+    call = build(nx, nz, ny, slots, levels, trunc, lon, half, width)
+    operands = [humidity, wind_east, wind_north, legendre, owner, vertical_modes, mode_values, table]
+    return call(*[pltpu.with_memory_space_constraint(v, pltpu.HBM) for v in operands])
 
 
 def solution(mesh):

time: 56 us -> 47.4 us (0.85)
  Pallas kernels: 52.6 us -> 46.4 us
  local copies, waits for them, and re-layouts: 3.2 us -> 0.83 us
    pallas_call x1, Pallas kernels: 52.6 us -> 46.4 us  [body(): call(*[pltpu.with_memory_space_constraint(v, pltpu.HBM) for v in operands])]
    reshape x1 -> x0, local copies, waits for them, and re-layouts: 1.27 us -> none  [body(): owner.reshape(1, trunc)]
    unnamed x1, local copies, waits for them, and re-layouts: 1.94 us -> 0.83 us
where the time goes in v2:
time: 47.4 us; the launch traced here: 47.2 us
  Pallas kernels  46.4 us (98%)
  local copies, waits for them, and re-layouts  0.83 us (2%)
    pallas_call x1, Pallas kernels, body(): call(*[pltpu.with_memory_space_constraint(v, pltpu.HBM) for v in operands])  46.4 us

profile of v2, /device:TPU:1, one launch (start us, length us, event | category | flops | bytes accessed | tf_op | source)
XLA Modules:
  0.0 47.2 jit_solution(3390330151541048519)
XLA Ops:
  0.0 46.4 %shard_map.82 = f32[10,40,384]{2,1,0:T(8,128)S(1)} custom-call(bf16[4,2,2560]{2,1,0:T(2,128)(2,1)} %hum_hbm.1, bf16[4,2,2560]{2,1,0:T(2,128)(2,1)} %east_hbm.1, bf16[4,2,2560]{2,1,0:T(2,128)(2,1)} %north_hbm.1, bf16[10,640,128]{2,1,0:T(8,128)(2,1)} %leg_ref.1, s32[640]{0:T(1024)} %owner_hbm.1, f32[64,64]{1,0:T(8,128)} %modes_hbm.1, f32[64]{0:T(128)} %values_hbm.1, ...), custom_call_target="tpu_custom_call" | custom-call | tf_op jit(solution)/shard_map/pallas_call | solution.py:495
  46.4 0.8 %copy.10 = f32[10,40,384]{2,1,0:T(8,128)} copy(f32[10,40,384]{2,1,0:T(8,128)S(1)} %shard_map.82) | data formatting | bytes 1228800

commit v3 on v2

--- a/solution.py
+++ b/solution.py
@@ -42,6 +42,10 @@
     top = np.concatenate([cos, -sin], axis=2)
     bottom = np.concatenate([sin * flip, cos * flip], axis=2)
     return np.concatenate([top, bottom], axis=1)
+
+
+def far_first(size):
+    return sorted(range(1, size), key=lambda i: -min(i, size - i))
 
 
 def place(rel, side):
@@ -124,6 +128,8 @@
     piece = 2 * fields * levels
     rows = slots * piece
     width = out_buf.shape[1]
+    wide = width // 2
+    half_slots = slots // 2
     lats = nx * nz * 2
     total_levels = ny * CORES * levels
     flat = 2 * fields * total_levels
@@ -140,12 +146,6 @@
         return {"lev": ((y + i) % ny) * CORES + core}
 
     partner = {"lev": y * CORES + 1 - core}
-
-    barrier = pltpu.get_barrier_semaphore()
-    peers = [along_x(i) for i in range(1, nx)] + [along_z(i) for i in range(1, nz)]
-    peers += [along_y(1), along_y(ny - 1), along_y(2), along_y(ny - 2), partner]
-    for peer in peers:
-        pl.semaphore_signal(barrier, inc=1, device_id=peer, device_id_type=MESH)
 
     loads = []
     for k, (source, target) in enumerate((
@@ -154,6 +154,11 @@
     )):
         loads.append(pltpu.make_async_copy(source, target, load_sem.at[k]))
         loads[-1].start()
+    barrier = pltpu.get_barrier_semaphore()
+    peers = [along_x(i) for i in far_first(nx)] + [along_z(i) for i in far_first(nz)]
+    peers += [along_y(2), along_y(ny - 2), along_y(1), along_y(ny - 1), partner]
+    for peer in peers:
+        pl.semaphore_signal(barrier, inc=1, device_id=peer, device_id_type=MESH)
     leg_copy = pltpu.make_async_copy(
         leg_ref.at[:, pl.ds(pl.multiple_of(lev * block, 8), block), :], leg_raw, leg_sem
     )
@@ -227,9 +232,11 @@
         spread.append(dot(pick, spectrum))
     halves = []
     for t in range(2):
-        pieces = [
-            jnp.where(rank_lane == float(s), spread[t], 0.0) for s in range(slots)
-        ] + [jnp.zeros((width - rows, trunc), F32)]
+        pieces = []
+        for s in range(slots):
+            pieces.append(jnp.where(rank_lane == float(s), spread[t], 0.0))
+            if (s + 1) % half_slots == 0 and wide > half_slots * piece:
+                pieces.append(jnp.zeros((wide - half_slots * piece, trunc), F32))
         halves.append(jnp.concatenate(pieces, axis=0))
     right = jnp.concatenate(halves, axis=1).astype(BF16)
     row = iota((2 * owners, trunc), 0).astype(F32)
@@ -245,7 +252,7 @@
     pl.semaphore_wait(barrier, len(peers))
 
     copies = []
-    for i in range(1, nx):
+    for i in far_first(nx):
         to = (x + i) % nx
         copy = pltpu.make_async_remote_copy(
             src_ref=out_buf.at[pl.ds(pl.multiple_of(to * bundle, bundle), bundle)],
@@ -262,43 +269,30 @@
     ]
 
     leg_copy.wait()
-    arrive = iota((lats, lats), 1)
-    from_z = arrive // bundle_z
-    from_x = (arrive % bundle_z) // 2
-    reach = one_hot(iota((lats, lats), 0) == (from_x * nz + from_z) * 2 + arrive % 2)
+    lane = iota((lats, lats), 1)
+    arrive = lane % owners
     leg = leg_raw[...].astype(F32).reshape(slots * block, lats).astype(BF16)
-    leg = dot(leg, reach)
     degree = iota((block, lats), 0).astype(F32) + (lev * block).astype(F32)
-    for s in range(slots):
-        live = degree >= own_waves[s : s + 1, :]
-        leg_buf[block * s : block * (s + 1), :] = jnp.where(
-            live, leg[block * s : block * (s + 1)], 0.0
-        )
+    for h in range(2):
+        from_z = arrive // bundle_z + h * (nz // 2)
+        from_x = (arrive % bundle_z) // 2
+        reach = iota((lats, lats), 0) == (from_x * nz + from_z) * 2 + arrive % 2
+        for part in range(2):
+            span = half_slots * block
+            turned = dot(
+                leg[part * span : (part + 1) * span], one_hot(reach & (lane // owners == part))
+            )
+            for k in range(half_slots):
+                s = part * half_slots + k
+                live = degree >= own_waves[s : s + 1, :]
+                leg_buf[h, block * s : block * (s + 1), :] = jnp.where(
+                    live, turned[block * k : block * (k + 1)], 0.0
+                )
 
     swap_to = iota((2 * owners, 2 * owners), 0)
     swap_from = iota((2 * owners, 2 * owners), 1)
     part_z, part_x, part_t = swap_to // bundle_z, (swap_to % bundle_z) // 2, swap_to % 2
     swap = one_hot(swap_from == part_x * bundle + part_z * 2 + part_t)
-
-    for copy in copies:
-        copy.wait_recv()
-    z_send[...] = dot(swap, x_buf[...]).astype(BF16)
-    copies_z = []
-    for i in range(1, nz):
-        to = (z + i) % nz
-        copy = pltpu.make_async_remote_copy(
-            src_ref=z_send.at[pl.ds(pl.multiple_of(to * bundle_z, bundle_z), bundle_z)],
-            dst_ref=z_buf.at[pl.ds(pl.multiple_of(z * bundle_z, bundle_z), bundle_z)],
-            send_sem=z_send_sem.at[i],
-            recv_sem=z_recv.at[i],
-            device_id=along_z(i),
-            device_id_type=MESH,
-        )
-        copy.start()
-        copies_z.append(copy)
-    z_buf[pl.ds(pl.multiple_of(z * bundle_z, bundle_z), bundle_z), :] = z_send[
-        pl.ds(pl.multiple_of(z * bundle_z, bundle_z), bundle_z), :
-    ]
 
     loads[5].wait()
     loads[6].wait()
@@ -325,9 +319,9 @@
     level64 = level64 - floor_div(level64, levels) * levels + jnp.concatenate(bases, axis=0)
     gather = one_hot(level64 == iota((flat, tl), 1).astype(F32))
     for k, part in enumerate((modes_high, modes_low)):
-        wide = dot(part, tile).astype(BF16)
+        stretched = dot(part, tile).astype(BF16)
         first_buf[k] = jnp.where(
-            row_part == column_part.astype(F32), dot(gather, wide), 0.0
+            row_part == column_part.astype(F32), dot(gather, stretched), 0.0
         ).astype(BF16)
         tall = dot(tile, part, (0, 1)).astype(BF16)
         last_buf[k] = jnp.where(row_id // tl == column_part, dot(tall, tile), 0.0).astype(BF16)
@@ -336,93 +330,136 @@
     shift = 4.0 * number * (number + 1.0) / (trunc * trunc)
     scale_buf[...] = 1.0 / (1.0 + shift * values)
 
-    for copy in copies_z:
+    for copy in copies:
         copy.wait_recv()
-    own = z_buf[...].astype(F32).T
-    y_buf[place(0, 0)] = own[:rows].astype(BF16)
+    z_send[...] = dot(swap, x_buf[...]).astype(BF16)
+    copies_z = []
+    for i in far_first(nz):
+        to = (z + i) % nz
+        copy = pltpu.make_async_remote_copy(
+            src_ref=z_send.at[pl.ds(pl.multiple_of(to * bundle_z, bundle_z), bundle_z)],
+            dst_ref=z_buf.at[pl.ds(pl.multiple_of(z * bundle_z, bundle_z), bundle_z)],
+            send_sem=z_send_sem.at[i],
+            recv_sem=z_recv.at[z],
+            device_id=along_z(i),
+            device_id_type=MESH,
+        )
+        copy.start()
+        copies_z.append(copy)
+    z_buf[pl.ds(pl.multiple_of(z * bundle_z, bundle_z), bundle_z), :] = z_send[
+        pl.ds(pl.multiple_of(z * bundle_z, bundle_z), bundle_z), :
+    ]
 
     pending = []
-    half = cfg["half"]
-
-    def message(k, rel, to, to_rel, side, start=0, size=rows):
+    cut = cfg["cut"]
+
+    def fill(h):
+        for source in range(h * nz // 2, (h + 1) * nz // 2):
+            @pl.when(source != z)
+            def _():
+                view = z_buf.at[pl.ds(source * bundle_z, bundle_z)]
+                pltpu.make_async_remote_copy(
+                    src_ref=view, dst_ref=view, send_sem=z_send_sem.at[0],
+                    recv_sem=z_recv.at[source], device_id=partner, device_id_type=MESH,
+                ).wait_recv()
+
+        own = z_buf[owners * h : owners * (h + 1), :].astype(F32)
+        own = jnp.concatenate([own[:, :wide], own[:, wide:]], axis=0)
+        y_buf[h, place(0, 0)] = own.T.astype(BF16)
+
+    def message(h, k, rel, to, to_rel, side, start=0, size=wide):
         return pltpu.make_async_remote_copy(
-            src_ref=y_buf.at[place(rel, 0), pl.ds(start, size)],
-            dst_ref=y_buf.at[place(to_rel, side), pl.ds(start, size)],
-            send_sem=y_send.at[k],
-            recv_sem=y_recv.at[k],
+            src_ref=y_buf.at[h, place(rel, 0), pl.ds(start, size)],
+            dst_ref=y_buf.at[h, place(to_rel, side), pl.ds(start, size)],
+            send_sem=y_send.at[h, k],
+            recv_sem=y_recv.at[h, k],
             device_id=to,
             device_id_type=MESH,
         )
 
-    def send(k, rel, step, start=0, size=rows):
-        copy = message(k, rel, along_y(step % ny), (rel - step) % ny, 0, start, size)
+    def send(h, k, rel, step, start=0, size=wide):
+        copy = message(h, k, rel, along_y(step % ny), (rel - step) % ny, 0, start, size)
         copy.start()
         pending.append(copy)
 
-    def hand(k, rel):
-        copy = message(k, rel, partner, rel, 1)
+    def hand(h, k, rel):
+        copy = message(h, k, rel, partner, rel, 1)
         copy.start()
         pending.append(copy)
 
-    def arrive_from(k, rel, side, start=0, size=rows):
+    def arrival(h, k, rel, side, start=0, size=wide):
+        view = y_buf.at[h, place(rel, side), pl.ds(start, size)]
         pltpu.make_async_remote_copy(
-            src_ref=y_buf.at[place(rel, side), pl.ds(start, size)],
-            dst_ref=y_buf.at[place(rel, side), pl.ds(start, size)],
-            send_sem=y_send.at[k],
-            recv_sem=y_recv.at[k],
-            device_id=partner,
-            device_id_type=MESH,
+            src_ref=view, dst_ref=view, send_sem=y_send.at[h, k], recv_sem=y_recv.at[h, k],
+            device_id=partner, device_id_type=MESH,
         ).wait_recv()
 
-    send(0, 0, 2)
-    send(1, 0, -2)
-    send(2, 0, 1)
-    send(3, 0, -1)
-    hand(8, 0)
-    arrive_from(0, ny - 2, 0)
-    send(4, ny - 2, 2, 0, half)
-    send(5, ny - 2, 1)
-    arrive_from(1, 2, 0)
-    send(6, 2, -2, half, rows - half)
-    send(7, 2, -1)
-    hand(9, ny - 2)
-    hand(10, 2)
-    arrive_from(2, ny - 1, 0)
-    hand(11, ny - 1)
-    arrive_from(3, 1, 0)
-    hand(12, 1)
-    arrive_from(8, 0, 1)
-    arrive_from(9, ny - 2, 1)
-    arrive_from(10, 2, 1)
-    arrive_from(11, ny - 1, 1)
-    arrive_from(12, 1, 1)
-
-    def modal_part(first, last):
+    def first_step(h):
+        send(h, 0, 0, 2)
+        send(h, 1, 0, -2)
+        send(h, 2, 0, 1)
+        send(h, 3, 0, -1)
+        hand(h, 8, 0)
+
+    def second_step(h):
+        arrival(h, 0, ny - 2, 0)
+        send(h, 4, ny - 2, 2, 0, cut)
+        send(h, 5, ny - 2, 1)
+        arrival(h, 1, 2, 0)
+        send(h, 6, 2, -2, cut, wide - cut)
+        send(h, 7, 2, -1)
+        hand(h, 9, ny - 2)
+        hand(h, 10, 2)
+        arrival(h, 2, ny - 1, 0)
+        hand(h, 11, ny - 1)
+        arrival(h, 3, 1, 0)
+        hand(h, 12, 1)
+
+    def last_step(h):
+        arrival(h, 5, ny - 3, 0)
+        hand(h, 13, ny - 3)
+        arrival(h, 7, 3, 0)
+        hand(h, 14, 3)
+        arrival(h, 4, 4, 0, 0, cut)
+        arrival(h, 6, 4, 0, cut, wide - cut)
+        hand(h, 15, 4)
+
+    def near_handed(h):
+        for k, rel in ((8, 0), (9, ny - 2), (10, 2), (11, ny - 1), (12, 1)):
+            arrival(h, k, rel, 1)
+
+    def far_handed(h):
+        for k, rel in ((13, ny - 3), (14, 3), (15, 4)):
+            arrival(h, k, rel, 1)
+
+    def modal_part(h, first, last):
         pieces = []
         for s in range(slots):
-            right = jnp.concatenate(
-                [y_buf[g, piece * s : piece * (s + 1), :] for g in range(first, last)], axis=0
-            )
-            left = leg_buf[block * s : block * (s + 1), :].astype(BF16)
+            rows_of = slice(piece * (s % half_slots), piece * (s % half_slots + 1))
+            right = jnp.concatenate([y_buf[h, g, rows_of, :] for g in range(first, last)], axis=0)
+            left = leg_buf[h, block * s : block * (s + 1), :].astype(BF16)
             pieces.append(dot(left, right, (1, 1)))
         projected = jnp.concatenate(pieces, axis=0).astype(BF16)
         span = slice(first * piece, last * piece)
         return dot(projected, first_buf[0, span, :]) + dot(projected, first_buf[1, span, :])
 
     near, groups = 10, ny * CORES
-    modal_buf[...] = modal_part(0, near)
-    arrive_from(5, ny - 3, 0)
-    hand(13, ny - 3)
-    arrive_from(7, 3, 0)
-    hand(14, 3)
-    arrive_from(4, 4, 0, 0, half)
-    arrive_from(6, 4, 0, half, rows - half)
-    hand(15, 4)
-    modal_buf[...] += modal_part(near, near + 3)
-    arrive_from(13, ny - 3, 1)
-    arrive_from(14, 3, 1)
-    arrive_from(15, 4, 1)
-    modal = modal_buf[...] + modal_part(near + 3, groups)
+    fill(0)
+    first_step(0)
+    second_step(0)
+    fill(1)
+    first_step(1)
+    last_step(0)
+    second_step(1)
+    near_handed(0)
+    far_handed(0)
+    modal_buf[...] = modal_part(0, 0, groups)
+    near_handed(1)
+    modal_buf[...] += modal_part(1, 0, near)
+    last_step(1)
+    modal_buf[...] += modal_part(1, near, near + 3)
+    far_handed(1)
+    modal = modal_buf[...] + modal_part(1, near + 3, groups)
     scale = jnp.concatenate([scale_buf[...]] * slots, axis=0)
     modal = (modal * scale).astype(BF16)
     solved = dot(modal, last_buf[0]) + dot(modal, last_buf[1])
@@ -432,16 +469,15 @@
         copy.wait_send()
 
 
-def build(nx, nz, ny, slots, levels, trunc, lon, half, width):
+def build(nx, nz, ny, slots, levels, trunc, lon, cut, width):
     block = trunc // (ny * CORES)
-    rows = slots * 6 * levels
     total_levels = levels * ny * CORES
     flat = 6 * total_levels
     lats = nx * nz * 2
     inner, units = lon // RADIX, trunc // RADIX
     cfg = dict(
         nx=nx, nz=nz, ny=ny, slots=slots, levels=levels, trunc=trunc, lon=lon, block=block,
-        half=half,
+        cut=cut,
     )
     dma = pltpu.SemaphoreType.DMA
     hbm = pl.BlockSpec(memory_space=pltpu.HBM)
@@ -462,14 +498,14 @@
             pltpu.VMEM((lats, width), BF16),
             pltpu.VMEM((lats, width), BF16),
             pltpu.VMEM((lats, width), BF16),
-            pltpu.VMEM((ny * CORES, rows, lats), BF16),
+            pltpu.VMEM((2, ny * CORES, width // 2, lats), BF16),
             pltpu.VMEM((slots, block, lats), BF16),
-            pltpu.VMEM((slots * block, lats), F32),
+            pltpu.VMEM((2, slots * block, lats), F32),
             pltpu.VMEM((2, flat, flat), BF16),
             pltpu.VMEM((2, flat, flat), BF16),
             pltpu.VMEM((block, flat), F32),
             pltpu.VMEM((slots * block, flat), F32),
-            dma((7,)), dma, dma((nx,)), dma((nx,)), dma((nz,)), dma((nz,)), dma((16,)), dma((16,)),
+            dma((7,)), dma, dma((nx,)), dma((nx,)), dma((nz,)), dma((nz,)), dma((2, 16)), dma((2, 16)),
         ],
         compiler_params=pltpu.CompilerParams(
             collective_id=0, has_side_effects=True, vmem_limit_bytes=VMEM_LIMIT
@@ -485,12 +521,12 @@
     ny = lax.axis_size("lev") // CORES
     slots = legendre.shape[0]
     rows = slots * 6 * levels
-    half = -(-rows // 32) * 16
-    width = -(-rows // 128) * 128
+    width = 2 * (-(-rows // 256) * 128)
+    cut = width // 4
     table = fourier_table(lon, trunc // RADIX)
     high = table.astype(BF16)
     table = jnp.asarray(np.concatenate([high, (table - high.astype(np.float64)).astype(BF16)]))
-    call = build(nx, nz, ny, slots, levels, trunc, lon, half, width)
+    call = build(nx, nz, ny, slots, levels, trunc, lon, cut, width)
     operands = [humidity, wind_east, wind_north, legendre, owner, vertical_modes, mode_values, table]
     return call(*[pltpu.with_memory_space_constraint(v, pltpu.HBM) for v in operands])
 

time: 47.4 us -> 50.1 us (1.057)
  Pallas kernels: 46.4 us -> 49.1 us
    pallas_call x1, Pallas kernels: 46.4 us -> 49.1 us  [body(): call(*[pltpu.with_memory_space_constraint(v, pltpu.HBM) for v in operands])]
where the time goes in v3:
time: 50.1 us; the launch traced here: 49.9 us
  Pallas kernels  49.1 us (98%)
  local copies, waits for them, and re-layouts  0.83 us (2%)
    pallas_call x1, Pallas kernels, body(): call(*[pltpu.with_memory_space_constraint(v, pltpu.HBM) for v in operands])  49.1 us

profile of v3, /device:TPU:1, one launch (start us, length us, event | category | flops | bytes accessed | tf_op | source)
XLA Modules:
  0.0 49.9 jit_solution(10211023448758799307)
XLA Ops:
  0.0 49.1 %shard_map.82 = f32[10,40,384]{2,1,0:T(8,128)S(1)} custom-call(bf16[4,2,2560]{2,1,0:T(2,128)(2,1)} %hum_hbm.1, bf16[4,2,2560]{2,1,0:T(2,128)(2,1)} %east_hbm.1, bf16[4,2,2560]{2,1,0:T(2,128)(2,1)} %north_hbm.1, bf16[10,640,128]{2,1,0:T(8,128)(2,1)} %leg_ref.1, s32[640]{0:T(1024)} %owner_hbm.1, f32[64,64]{1,0:T(8,128)} %modes_hbm.1, f32[64]{0:T(128)} %values_hbm.1, ...), custom_call_target="tpu_custom_call" | custom-call | tf_op jit(solution)/shard_map/pallas_call | solution.py:531
  49.1 0.8 %copy.10 = f32[10,40,384]{2,1,0:T(8,128)} copy(f32[10,40,384]{2,1,0:T(8,128)S(1)} %shard_map.82) | data formatting | bytes 1228800

commit v4 on v2

--- a/solution.py
+++ b/solution.py
@@ -42,6 +42,10 @@
     top = np.concatenate([cos, -sin], axis=2)
     bottom = np.concatenate([sin * flip, cos * flip], axis=2)
     return np.concatenate([top, bottom], axis=1)
+
+
+def far_first(size):
+    return sorted(range(1, size), key=lambda i: -min(i, size - i))
 
 
 def place(rel, side):
@@ -141,12 +145,6 @@
 
     partner = {"lev": y * CORES + 1 - core}
 
-    barrier = pltpu.get_barrier_semaphore()
-    peers = [along_x(i) for i in range(1, nx)] + [along_z(i) for i in range(1, nz)]
-    peers += [along_y(1), along_y(ny - 1), along_y(2), along_y(ny - 2), partner]
-    for peer in peers:
-        pl.semaphore_signal(barrier, inc=1, device_id=peer, device_id_type=MESH)
-
     loads = []
     for k, (source, target) in enumerate((
         (owner_hbm, owner_ref), (hum_hbm, hum_ref), (east_hbm, east_ref), (north_hbm, north_ref),
@@ -154,6 +152,11 @@
     )):
         loads.append(pltpu.make_async_copy(source, target, load_sem.at[k]))
         loads[-1].start()
+    barrier = pltpu.get_barrier_semaphore()
+    peers = [along_x(i) for i in far_first(nx)] + [along_z(i) for i in far_first(nz)]
+    peers += [along_y(2), along_y(ny - 2), along_y(1), along_y(ny - 1), partner]
+    for peer in peers:
+        pl.semaphore_signal(barrier, inc=1, device_id=peer, device_id_type=MESH)
     leg_copy = pltpu.make_async_copy(
         leg_ref.at[:, pl.ds(pl.multiple_of(lev * block, 8), block), :], leg_raw, leg_sem
     )
@@ -245,7 +248,7 @@
     pl.semaphore_wait(barrier, len(peers))
 
     copies = []
-    for i in range(1, nx):
+    for i in far_first(nx):
         to = (x + i) % nx
         copy = pltpu.make_async_remote_copy(
             src_ref=out_buf.at[pl.ds(pl.multiple_of(to * bundle, bundle), bundle)],
@@ -279,26 +282,6 @@
     swap_from = iota((2 * owners, 2 * owners), 1)
     part_z, part_x, part_t = swap_to // bundle_z, (swap_to % bundle_z) // 2, swap_to % 2
     swap = one_hot(swap_from == part_x * bundle + part_z * 2 + part_t)
-
-    for copy in copies:
-        copy.wait_recv()
-    z_send[...] = dot(swap, x_buf[...]).astype(BF16)
-    copies_z = []
-    for i in range(1, nz):
-        to = (z + i) % nz
-        copy = pltpu.make_async_remote_copy(
-            src_ref=z_send.at[pl.ds(pl.multiple_of(to * bundle_z, bundle_z), bundle_z)],
-            dst_ref=z_buf.at[pl.ds(pl.multiple_of(z * bundle_z, bundle_z), bundle_z)],
-            send_sem=z_send_sem.at[i],
-            recv_sem=z_recv.at[i],
-            device_id=along_z(i),
-            device_id_type=MESH,
-        )
-        copy.start()
-        copies_z.append(copy)
-    z_buf[pl.ds(pl.multiple_of(z * bundle_z, bundle_z), bundle_z), :] = z_send[
-        pl.ds(pl.multiple_of(z * bundle_z, bundle_z), bundle_z), :
-    ]
 
     loads[5].wait()
     loads[6].wait()
@@ -336,6 +319,26 @@
     shift = 4.0 * number * (number + 1.0) / (trunc * trunc)
     scale_buf[...] = 1.0 / (1.0 + shift * values)
 
+    for copy in copies:
+        copy.wait_recv()
+    z_send[...] = dot(swap, x_buf[...]).astype(BF16)
+    copies_z = []
+    for i in far_first(nz):
+        to = (z + i) % nz
+        copy = pltpu.make_async_remote_copy(
+            src_ref=z_send.at[pl.ds(pl.multiple_of(to * bundle_z, bundle_z), bundle_z)],
+            dst_ref=z_buf.at[pl.ds(pl.multiple_of(z * bundle_z, bundle_z), bundle_z)],
+            send_sem=z_send_sem.at[i],
+            recv_sem=z_recv.at[i],
+            device_id=along_z(i),
+            device_id_type=MESH,
+        )
+        copy.start()
+        copies_z.append(copy)
+    z_buf[pl.ds(pl.multiple_of(z * bundle_z, bundle_z), bundle_z), :] = z_send[
+        pl.ds(pl.multiple_of(z * bundle_z, bundle_z), bundle_z), :
+    ]
+
     for copy in copies_z:
         copy.wait_recv()
     own = z_buf[...].astype(F32).T
@@ -357,45 +360,54 @@
     def send(k, rel, step, start=0, size=rows):
         copy = message(k, rel, along_y(step % ny), (rel - step) % ny, 0, start, size)
         copy.start()
-        pending.append(copy)
-
-    def hand(k, rel):
-        copy = message(k, rel, partner, rel, 1)
+        return copy
+
+    def relay(*args):
+        pending.append(send(*args))
+
+    def hand(k, rel, start=0, size=rows):
+        copy = message(k, rel, partner, rel, 1, start, size)
         copy.start()
         pending.append(copy)
 
     def arrive_from(k, rel, side, start=0, size=rows):
+        view = y_buf.at[place(rel, side), pl.ds(start, size)]
         pltpu.make_async_remote_copy(
-            src_ref=y_buf.at[place(rel, side), pl.ds(start, size)],
-            dst_ref=y_buf.at[place(rel, side), pl.ds(start, size)],
-            send_sem=y_send.at[k],
-            recv_sem=y_recv.at[k],
-            device_id=partner,
-            device_id_type=MESH,
+            src_ref=view, dst_ref=view, send_sem=y_send.at[k], recv_sem=y_recv.at[k],
+            device_id=partner, device_id_type=MESH,
         ).wait_recv()
 
-    send(0, 0, 2)
-    send(1, 0, -2)
-    send(2, 0, 1)
-    send(3, 0, -1)
-    hand(8, 0)
-    arrive_from(0, ny - 2, 0)
-    send(4, ny - 2, 2, 0, half)
-    send(5, ny - 2, 1)
-    arrive_from(1, 2, 0)
-    send(6, 2, -2, half, rows - half)
-    send(7, 2, -1)
-    hand(9, ny - 2)
-    hand(10, 2)
-    arrive_from(2, ny - 1, 0)
-    hand(11, ny - 1)
-    arrive_from(3, 1, 0)
-    hand(12, 1)
-    arrive_from(8, 0, 1)
-    arrive_from(9, ny - 2, 1)
-    arrive_from(10, 2, 1)
-    arrive_from(11, ny - 1, 1)
-    arrive_from(12, 1, 1)
+    lower, upper = (0, half), (half, rows - half)
+    below, above = ny - 2, 2
+    for up, down in ((lower, upper), (upper, lower)):
+        k = 0 if up == lower else 2
+        first = send(k, 0, 2, *up), send(k + 1, 0, -2, *down)
+        for copy in first:
+            copy.wait_send()
+    relay(4, 0, 1)
+    relay(5, 0, -1)
+    hand(12, 0)
+    arrive_from(0, below, 0, *lower)
+    relay(6, below, 2, *lower)
+    relay(8, below, 1, *lower)
+    arrive_from(1, above, 0, *upper)
+    relay(7, above, -2, *upper)
+    relay(9, above, -1, *upper)
+    arrive_from(2, below, 0, *upper)
+    relay(10, below, 1, *upper)
+    arrive_from(3, above, 0, *lower)
+    relay(11, above, -1, *lower)
+    hand(13, below)
+    hand(14, above)
+    arrive_from(4, ny - 1, 0)
+    hand(15, ny - 1)
+    arrive_from(5, 1, 0)
+    hand(16, 1)
+    arrive_from(12, 0, 1)
+    arrive_from(13, below, 1)
+    arrive_from(14, above, 1)
+    arrive_from(15, ny - 1, 1)
+    arrive_from(16, 1, 1)
 
     def modal_part(first, last):
         pieces = []
@@ -411,17 +423,23 @@
 
     near, groups = 10, ny * CORES
     modal_buf[...] = modal_part(0, near)
-    arrive_from(5, ny - 3, 0)
-    hand(13, ny - 3)
-    arrive_from(7, 3, 0)
-    hand(14, 3)
-    arrive_from(4, 4, 0, 0, half)
-    arrive_from(6, 4, 0, half, rows - half)
-    hand(15, 4)
+    arrive_from(6, 4, 0, *lower)
+    arrive_from(7, 4, 0, *upper)
+    hand(17, 4)
+    arrive_from(8, ny - 3, 0, *lower)
+    hand(18, ny - 3, *lower)
+    arrive_from(9, 3, 0, *upper)
+    hand(19, 3, *upper)
+    arrive_from(10, ny - 3, 0, *upper)
+    hand(20, ny - 3, *upper)
+    arrive_from(11, 3, 0, *lower)
+    hand(21, 3, *lower)
     modal_buf[...] += modal_part(near, near + 3)
-    arrive_from(13, ny - 3, 1)
-    arrive_from(14, 3, 1)
-    arrive_from(15, 4, 1)
+    arrive_from(17, 4, 1)
+    arrive_from(18, ny - 3, 1, *lower)
+    arrive_from(19, 3, 1, *upper)
+    arrive_from(20, ny - 3, 1, *upper)
+    arrive_from(21, 3, 1, *lower)
     modal = modal_buf[...] + modal_part(near + 3, groups)
     scale = jnp.concatenate([scale_buf[...]] * slots, axis=0)
     modal = (modal * scale).astype(BF16)
@@ -469,7 +487,7 @@
             pltpu.VMEM((2, flat, flat), BF16),
             pltpu.VMEM((block, flat), F32),
             pltpu.VMEM((slots * block, flat), F32),
-            dma((7,)), dma, dma((nx,)), dma((nx,)), dma((nz,)), dma((nz,)), dma((16,)), dma((16,)),
+            dma((7,)), dma, dma((nx,)), dma((nx,)), dma((nz,)), dma((nz,)), dma((22,)), dma((22,)),
         ],
         compiler_params=pltpu.CompilerParams(
             collective_id=0, has_side_effects=True, vmem_limit_bytes=VMEM_LIMIT

time: 47.4 us -> 46.1 us (0.973)
  Pallas kernels: 46.4 us -> 45.1 us
    pallas_call x1, Pallas kernels: 46.4 us -> 45.1 us  [body(): call(*[pltpu.with_memory_space_constraint(v, pltpu.HBM) for v in operands])]
where the time goes in v4:
time: 46.1 us; the launch traced here: 45.9 us
  Pallas kernels  45.1 us (98%)
  local copies, waits for them, and re-layouts  0.83 us (2%)
    pallas_call x1, Pallas kernels, body(): call(*[pltpu.with_memory_space_constraint(v, pltpu.HBM) for v in operands])  45.1 us

profile of v4, /device:TPU:1, one launch (start us, length us, event | category | flops | bytes accessed | tf_op | source)
XLA Modules:
  0.0 45.9 jit_solution(17841800670237522484)
XLA Ops:
  0.0 45.1 %shard_map.82 = f32[10,40,384]{2,1,0:T(8,128)S(1)} custom-call(bf16[4,2,2560]{2,1,0:T(2,128)(2,1)} %hum_hbm.1, bf16[4,2,2560]{2,1,0:T(2,128)(2,1)} %east_hbm.1, bf16[4,2,2560]{2,1,0:T(2,128)(2,1)} %north_hbm.1, bf16[10,640,128]{2,1,0:T(8,128)(2,1)} %leg_ref.1, s32[640]{0:T(1024)} %owner_hbm.1, f32[64,64]{1,0:T(8,128)} %modes_hbm.1, f32[64]{0:T(128)} %values_hbm.1, ...), custom_call_target="tpu_custom_call" | custom-call | tf_op jit(solution)/shard_map/pallas_call | solution.py:513
  45.1 0.8 %copy.10 = f32[10,40,384]{2,1,0:T(8,128)} copy(f32[10,40,384]{2,1,0:T(8,128)S(1)} %shard_map.82) | data formatting | bytes 1228800

commit v5 on v4

--- a/solution.py
+++ b/solution.py
@@ -113,7 +113,7 @@
     cfg, hum_hbm, east_hbm, north_hbm, leg_ref, owner_hbm, modes_hbm, values_hbm, table_hbm,
     out_ref,
     hum_ref, east_ref, north_ref, owner_ref, modes_ref, values_ref, table_ref,
-    out_buf, x_buf, z_send, z_buf, y_buf, leg_raw, leg_buf, first_buf, last_buf, scale_buf,
+    out_buf, x_buf, z_send, z_buf, y_buf, leg_raw, leg_buf, first_buf, late_buf, last_buf, scale_buf,
     modal_buf,
     load_sem, leg_sem, x_send, x_recv, z_send_sem, z_recv, y_send, y_recv,
 ):
@@ -186,7 +186,7 @@
     both = dot(both.astype(BF16), reorder)
     owner_lane, rank_lane = both[0:1], both[1:2]
 
-    for copy in loads[1:5]:
+    for copy in loads[1:4]:
         copy.wait()
     humidity = hum_ref[...].astype(F32).reshape(2 * levels, lon)
     east = east_ref[...].astype(F32).reshape(2 * levels, lon)
@@ -197,6 +197,7 @@
     real, imag = short_fourier(grid, inner)
     joined = [jnp.concatenate([r, i], axis=1) for r, i in zip(real, imag)]
     grid_rows = grid.shape[0]
+    loads[4].wait()
     reals, imags = [], []
     for p in range(RADIX // 4):
         table = table_ref[p]
@@ -307,13 +308,23 @@
             )
     level64 = level64 - floor_div(level64, levels) * levels + jnp.concatenate(bases, axis=0)
     gather = one_hot(level64 == iota((flat, tl), 1).astype(F32))
+    near, groups = 10, ny * CORES
+    pair = 2 * tl
+    late = (near + 3) * piece
+    padded = late_buf.shape[0] // 2
+    tile_pair = tile[:, :pair]
+    same = iota((pair, pair), 0) // tl == iota((pair, pair), 1) // tl
     for k, part in enumerate((modes_high, modes_low)):
-        wide = dot(part, tile).astype(BF16)
-        first_buf[k] = jnp.where(
-            row_part == column_part.astype(F32), dot(gather, wide), 0.0
+        stretched = dot(part, tile).astype(BF16)
+        first = jnp.where(row_part == column_part.astype(F32), dot(gather, stretched), 0.0)
+        first_buf[k] = first.astype(BF16)
+        late_buf[k * padded : (k + 1) * padded, :] = jnp.concatenate(
+            [first[late:], jnp.zeros((padded - flat + late, flat), F32)], axis=0
         ).astype(BF16)
-        tall = dot(tile, part, (0, 1)).astype(BF16)
-        last_buf[k] = jnp.where(row_id // tl == column_part, dot(tall, tile), 0.0).astype(BF16)
+        tall = dot(tile_pair, part, (0, 1)).astype(BF16)
+        last_buf[k * pair : (k + 1) * pair, :] = jnp.where(
+            same, dot(tall, tile_pair), 0.0
+        ).astype(BF16)
     values = jnp.concatenate([values_ref[...].reshape(1, tl)] * (2 * fields), axis=1)
     number = iota((block, flat), 0).astype(F32) + (lev * block).astype(F32)
     shift = 4.0 * number * (number + 1.0) / (trunc * trunc)
@@ -409,19 +420,21 @@
     arrive_from(15, ny - 1, 1)
     arrive_from(16, 1, 1)
 
-    def modal_part(first, last):
+    def project(first, last, padding):
         pieces = []
         for s in range(slots):
-            right = jnp.concatenate(
-                [y_buf[g, piece * s : piece * (s + 1), :] for g in range(first, last)], axis=0
-            )
+            blocks = [y_buf[g, piece * s : piece * (s + 1), :] for g in range(first, last)]
+            if padding:
+                blocks.append(jnp.zeros((padding, lats), BF16))
             left = leg_buf[block * s : block * (s + 1), :].astype(BF16)
-            pieces.append(dot(left, right, (1, 1)))
-        projected = jnp.concatenate(pieces, axis=0).astype(BF16)
+            pieces.append(dot(left, jnp.concatenate(blocks, axis=0), (1, 1)))
+        return jnp.concatenate(pieces, axis=0).astype(BF16)
+
+    def modal_part(first, last):
+        projected = project(first, last, 0)
         span = slice(first * piece, last * piece)
         return dot(projected, first_buf[0, span, :]) + dot(projected, first_buf[1, span, :])
 
-    near, groups = 10, ny * CORES
     modal_buf[...] = modal_part(0, near)
     arrive_from(6, 4, 0, *lower)
     arrive_from(7, 4, 0, *upper)
@@ -440,10 +453,15 @@
     arrive_from(19, 3, 1, *upper)
     arrive_from(20, ny - 3, 1, *upper)
     arrive_from(21, 3, 1, *lower)
-    modal = modal_buf[...] + modal_part(near + 3, groups)
+    projected = project(near + 3, groups, padded - flat + late)
+    modal = modal_buf[...] + dot(jnp.concatenate([projected, projected], axis=1), late_buf[...])
     scale = jnp.concatenate([scale_buf[...]] * slots, axis=0)
     modal = (modal * scale).astype(BF16)
-    solved = dot(modal, last_buf[0]) + dot(modal, last_buf[1])
+    solved = []
+    for j in range(flat // pair):
+        part = modal[:, j * pair : (j + 1) * pair]
+        solved.append(dot(jnp.concatenate([part, part], axis=1), last_buf[...]))
+    solved = jnp.concatenate(solved, axis=1)
     out_ref[...] = solved.reshape(slots, block, flat)
 
     for copy in copies + copies_z + pending:
@@ -484,7 +502,8 @@
             pltpu.VMEM((slots, block, lats), BF16),
             pltpu.VMEM((slots * block, lats), F32),
             pltpu.VMEM((2, flat, flat), BF16),
-            pltpu.VMEM((2, flat, flat), BF16),
+            pltpu.VMEM((2 * (-(-18 * levels // 128) * 128), flat), BF16),
+            pltpu.VMEM((4 * total_levels, 2 * total_levels), BF16),
             pltpu.VMEM((block, flat), F32),
             pltpu.VMEM((slots * block, flat), F32),
             dma((7,)), dma, dma((nx,)), dma((nx,)), dma((nz,)), dma((nz,)), dma((22,)), dma((22,)),

time: 46.1 us -> 45.9 us (level)
  no operation moved by 1% of the time
where the time goes in v5:
time: 45.9 us; the launch traced here: 45.7 us
  Pallas kernels  44.9 us (98%)
  local copies, waits for them, and re-layouts  0.83 us (2%)
    pallas_call x1, Pallas kernels, body(): call(*[pltpu.with_memory_space_constraint(v, pltpu.HBM) for v in operands])  44.9 us

profile of v5, /device:TPU:1, one launch (start us, length us, event | category | flops | bytes accessed | tf_op | source)
XLA Modules:
  0.0 45.7 jit_solution(17522569635842133686)
XLA Ops:
  0.0 44.9 %shard_map.82 = f32[10,40,384]{2,1,0:T(8,128)S(1)} custom-call(bf16[4,2,2560]{2,1,0:T(2,128)(2,1)} %hum_hbm.1, bf16[4,2,2560]{2,1,0:T(2,128)(2,1)} %east_hbm.1, bf16[4,2,2560]{2,1,0:T(2,128)(2,1)} %north_hbm.1, bf16[10,640,128]{2,1,0:T(8,128)(2,1)} %leg_ref.1, s32[640]{0:T(1024)} %owner_hbm.1, f32[64,64]{1,0:T(8,128)} %modes_hbm.1, f32[64]{0:T(128)} %values_hbm.1, ...), custom_call_target="tpu_custom_call" | custom-call | tf_op jit(solution)/shard_map/pallas_call | solution.py:532
  44.9 0.8 %copy.10 = f32[10,40,384]{2,1,0:T(8,128)} copy(f32[10,40,384]{2,1,0:T(8,128)S(1)} %shard_map.82) | data formatting | bytes 1228800

commit v6 on v5

--- a/solution.py
+++ b/solution.py
@@ -145,6 +145,11 @@
 
     partner = {"lev": y * CORES + 1 - core}
 
+    barrier = pltpu.get_barrier_semaphore()
+    peers = [along_x(i) for i in far_first(nx)] + [along_z(i) for i in far_first(nz)]
+    peers += [along_y(2), along_y(ny - 2), along_y(1), along_y(ny - 1), partner]
+    for peer in peers:
+        pl.semaphore_signal(barrier, inc=1, device_id=peer, device_id_type=MESH)
     loads = []
     for k, (source, target) in enumerate((
         (owner_hbm, owner_ref), (hum_hbm, hum_ref), (east_hbm, east_ref), (north_hbm, north_ref),
@@ -152,11 +157,6 @@
     )):
         loads.append(pltpu.make_async_copy(source, target, load_sem.at[k]))
         loads[-1].start()
-    barrier = pltpu.get_barrier_semaphore()
-    peers = [along_x(i) for i in far_first(nx)] + [along_z(i) for i in far_first(nz)]
-    peers += [along_y(2), along_y(ny - 2), along_y(1), along_y(ny - 1), partner]
-    for peer in peers:
-        pl.semaphore_signal(barrier, inc=1, device_id=peer, device_id_type=MESH)
     leg_copy = pltpu.make_async_copy(
         leg_ref.at[:, pl.ds(pl.multiple_of(lev * block, 8), block), :], leg_raw, leg_sem
     )
@@ -390,11 +390,10 @@
 
     lower, upper = (0, half), (half, rows - half)
     below, above = ny - 2, 2
-    for up, down in ((lower, upper), (upper, lower)):
-        k = 0 if up == lower else 2
-        first = send(k, 0, 2, *up), send(k + 1, 0, -2, *down)
-        for copy in first:
-            copy.wait_send()
+    relay(0, 0, 2, *lower)
+    relay(1, 0, -2, *upper)
+    relay(2, 0, 2, *upper)
+    relay(3, 0, -2, *lower)
     relay(4, 0, 1)
     relay(5, 0, -1)
     hand(12, 0)
@@ -436,13 +435,13 @@
         return dot(projected, first_buf[0, span, :]) + dot(projected, first_buf[1, span, :])
 
     modal_buf[...] = modal_part(0, near)
-    arrive_from(6, 4, 0, *lower)
-    arrive_from(7, 4, 0, *upper)
-    hand(17, 4)
     arrive_from(8, ny - 3, 0, *lower)
     hand(18, ny - 3, *lower)
     arrive_from(9, 3, 0, *upper)
     hand(19, 3, *upper)
+    arrive_from(6, 4, 0, *lower)
+    arrive_from(7, 4, 0, *upper)
+    hand(17, 4)
     arrive_from(10, ny - 3, 0, *upper)
     hand(20, ny - 3, *upper)
     arrive_from(11, 3, 0, *lower)

time: 45.9 us -> 45.5 us (level)
  no operation moved by 1% of the time
where the time goes in v6:
time: 45.5 us; the launch traced here: 45.4 us
  Pallas kernels  44.5 us (98%)
  local copies, waits for them, and re-layouts  0.83 us (2%)
    pallas_call x1, Pallas kernels, body(): call(*[pltpu.with_memory_space_constraint(v, pltpu.HBM) for v in operands])  44.5 us

profile of v6, /device:TPU:1, one launch (start us, length us, event | category | flops | bytes accessed | tf_op | source)
XLA Modules:
  0.0 45.4 jit_solution(2993887464129281849)
XLA Ops:
  0.0 44.5 %shard_map.82 = f32[10,40,384]{2,1,0:T(8,128)S(1)} custom-call(bf16[4,2,2560]{2,1,0:T(2,128)(2,1)} %hum_hbm.1, bf16[4,2,2560]{2,1,0:T(2,128)(2,1)} %east_hbm.1, bf16[4,2,2560]{2,1,0:T(2,128)(2,1)} %north_hbm.1, bf16[10,640,128]{2,1,0:T(8,128)(2,1)} %leg_ref.1, s32[640]{0:T(1024)} %owner_hbm.1, f32[64,64]{1,0:T(8,128)} %modes_hbm.1, f32[64]{0:T(128)} %values_hbm.1, ...), custom_call_target="tpu_custom_call" | custom-call | tf_op jit(solution)/shard_map/pallas_call | solution.py:531
  44.5 0.8 %copy.10 = f32[10,40,384]{2,1,0:T(8,128)} copy(f32[10,40,384]{2,1,0:T(8,128)S(1)} %shard_map.82) | data formatting | bytes 1228800

commit v7 on v6

--- a/solution.py
+++ b/solution.py
@@ -389,35 +389,33 @@
         ).wait_recv()
 
     lower, upper = (0, half), (half, rows - half)
+    step = half // 2
+    parts = [(0, step), (step, half - step), (half, step), (half + step, rows - half - step)]
     below, above = ny - 2, 2
-    relay(0, 0, 2, *lower)
-    relay(1, 0, -2, *upper)
-    relay(2, 0, 2, *upper)
-    relay(3, 0, -2, *lower)
-    relay(4, 0, 1)
-    relay(5, 0, -1)
-    hand(12, 0)
-    arrive_from(0, below, 0, *lower)
-    relay(6, below, 2, *lower)
-    relay(8, below, 1, *lower)
-    arrive_from(1, above, 0, *upper)
-    relay(7, above, -2, *upper)
-    relay(9, above, -1, *upper)
-    arrive_from(2, below, 0, *upper)
-    relay(10, below, 1, *upper)
-    arrive_from(3, above, 0, *lower)
-    relay(11, above, -1, *lower)
-    hand(13, below)
-    hand(14, above)
-    arrive_from(4, ny - 1, 0)
-    hand(15, ny - 1)
-    arrive_from(5, 1, 0)
-    hand(16, 1)
-    arrive_from(12, 0, 1)
-    arrive_from(13, below, 1)
-    arrive_from(14, above, 1)
-    arrive_from(15, ny - 1, 1)
-    arrive_from(16, 1, 1)
+    rise, fall = (0, 1, 2, 3), (2, 3, 0, 1)
+    for i, j in zip(rise, fall):
+        relay(i, 0, 2, *parts[i])
+        relay(4 + j, 0, -2, *parts[j])
+    relay(8, 0, 1)
+    relay(9, 0, -1)
+    hand(22, 0)
+    for i, j in zip(rise, fall):
+        arrive_from(i, below, 0, *parts[i])
+        if i < 2:
+            relay(10 + i, below, 2, *parts[i])
+        relay(14 + i, below, 1, *parts[i])
+        arrive_from(4 + j, above, 0, *parts[j])
+        if j >= 2:
+            relay(10 + j, above, -2, *parts[j])
+        relay(18 + j, above, -1, *parts[j])
+    hand(23, below)
+    hand(24, above)
+    arrive_from(8, ny - 1, 0)
+    hand(25, ny - 1)
+    arrive_from(9, 1, 0)
+    hand(26, 1)
+    for k, rel in ((22, 0), (23, below), (24, above), (25, ny - 1), (26, 1)):
+        arrive_from(k, rel, 1)
 
     def project(first, last, padding):
         pieces = []
@@ -435,23 +433,27 @@
         return dot(projected, first_buf[0, span, :]) + dot(projected, first_buf[1, span, :])
 
     modal_buf[...] = modal_part(0, near)
-    arrive_from(8, ny - 3, 0, *lower)
-    hand(18, ny - 3, *lower)
-    arrive_from(9, 3, 0, *upper)
-    hand(19, 3, *upper)
-    arrive_from(6, 4, 0, *lower)
-    arrive_from(7, 4, 0, *upper)
-    hand(17, 4)
-    arrive_from(10, ny - 3, 0, *upper)
-    hand(20, ny - 3, *upper)
-    arrive_from(11, 3, 0, *lower)
-    hand(21, 3, *lower)
+    for i in (0, 1):
+        arrive_from(14 + i, ny - 3, 0, *parts[i])
+    hand(28, ny - 3, *lower)
+    for i in (2, 3):
+        arrive_from(18 + i, 3, 0, *parts[i])
+    hand(29, 3, *upper)
+    for i in range(4):
+        arrive_from(10 + i, 4, 0, *parts[i])
+    hand(27, 4)
+    for i in (2, 3):
+        arrive_from(14 + i, ny - 3, 0, *parts[i])
+    hand(30, ny - 3, *upper)
+    for i in (0, 1):
+        arrive_from(18 + i, 3, 0, *parts[i])
+    hand(31, 3, *lower)
     modal_buf[...] += modal_part(near, near + 3)
-    arrive_from(17, 4, 1)
-    arrive_from(18, ny - 3, 1, *lower)
-    arrive_from(19, 3, 1, *upper)
-    arrive_from(20, ny - 3, 1, *upper)
-    arrive_from(21, 3, 1, *lower)
+    arrive_from(27, 4, 1)
+    arrive_from(28, ny - 3, 1, *lower)
+    arrive_from(29, 3, 1, *upper)
+    arrive_from(30, ny - 3, 1, *upper)
+    arrive_from(31, 3, 1, *lower)
     projected = project(near + 3, groups, padded - flat + late)
     modal = modal_buf[...] + dot(jnp.concatenate([projected, projected], axis=1), late_buf[...])
     scale = jnp.concatenate([scale_buf[...]] * slots, axis=0)
@@ -505,7 +507,7 @@
             pltpu.VMEM((4 * total_levels, 2 * total_levels), BF16),
             pltpu.VMEM((block, flat), F32),
             pltpu.VMEM((slots * block, flat), F32),
-            dma((7,)), dma, dma((nx,)), dma((nx,)), dma((nz,)), dma((nz,)), dma((22,)), dma((22,)),
+            dma((7,)), dma, dma((nx,)), dma((nx,)), dma((nz,)), dma((nz,)), dma((32,)), dma((32,)),
         ],
         compiler_params=pltpu.CompilerParams(
             collective_id=0, has_side_effects=True, vmem_limit_bytes=VMEM_LIMIT

time: 45.5 us -> 45.4 us (level)
  no operation moved by 1% of the time
where the time goes in v7:
time: 45.4 us; the launch traced here: 45.3 us
  Pallas kernels  44.4 us (98%)
  local copies, waits for them, and re-layouts  0.83 us (2%)
    pallas_call x1, Pallas kernels, body(): call(*[pltpu.with_memory_space_constraint(v, pltpu.HBM) for v in operands])  44.4 us

profile of v7, /device:TPU:1, one launch (start us, length us, event | category | flops | bytes accessed | tf_op | source)
XLA Modules:
  0.0 45.3 jit_solution(11136267588406891638)
XLA Ops:
  0.0 44.4 %shard_map.82 = f32[10,40,384]{2,1,0:T(8,128)S(1)} custom-call(bf16[4,2,2560]{2,1,0:T(2,128)(2,1)} %hum_hbm.1, bf16[4,2,2560]{2,1,0:T(2,128)(2,1)} %east_hbm.1, bf16[4,2,2560]{2,1,0:T(2,128)(2,1)} %north_hbm.1, bf16[10,640,128]{2,1,0:T(8,128)(2,1)} %leg_ref.1, s32[640]{0:T(1024)} %owner_hbm.1, f32[64,64]{1,0:T(8,128)} %modes_hbm.1, f32[64]{0:T(128)} %values_hbm.1, ...), custom_call_target="tpu_custom_call" | custom-call | tf_op jit(solution)/shard_map/pallas_call | solution.py:533
  44.5 0.8 %copy.10 = f32[10,40,384]{2,1,0:T(8,128)} copy(f32[10,40,384]{2,1,0:T(8,128)S(1)} %shard_map.82) | data formatting | bytes 1228800
